TPU v7x, 256 devices: a whole 4x4x8 slice. The times are simulated.
256 devices in a mesh: rec: 8 (over y, core), tm: 32 (over x, z).
Axes of the slice: x: 4, y: 4, z: 8, core: 2. Of those that a mesh axis runs over, the one named last changes fastest.
Arguments:
- frames: bfloat16 [8, 16384, 1024], P('rec', 'tm'), may hold values from -6 to 6
- lengths: int32 [8], P('rec'), may hold values from 4096 to 16384, as said below
- norm_gain: float32 [1024], replicated, may hold values from 0.1 to 1.9
- memory_gain: float32 [1024], replicated, may hold values from 0.1 to 1.9
- qkv_weight: bfloat16 [3, 1024, 1024], P(None, None, 'tm'), may hold values from -3.75 to 3.75
- out_weight: bfloat16 [1024, 1024], P(None, 'tm'), may hold values from -0.1875 to 0.1875
- segment_ids: int32 [8, 32, 512], P('rec', 'tm'), may hold values from 0 to 127, never falling along the last dimension, each value on 1 to 12 neighbouring positions
- owners: int32 [8, 32, 128, 1], P('rec', 'tm'), may hold values from 0 to 31; in each aligned block of 128 rows (0 to 127, 128 to 255, ..., all dimensions but the last counted through in order) at most 8 rows name the same one
- language_weight: bfloat16 [1024, 2048], P(None, 'rec'), may hold values from -0.1875 to 0.1875
Outputs:
- encoded: bfloat16 [8, 16384, 1024], P('rec', 'tm')
- lm_rows: bfloat16 [8, 32, 256, 2048], P('rec', 'tm')
Inputs may be any that keep to these rules, and one draw needn't show every extreme that they name: `lengths`: one recording has exactly 16384 live frames. `segment_ids`: in each block, token numbers never fall and each of the 128 tokens has 1 to 12 frames, one exactly 12. `owners`: within the 128 tokens of one block no owner is named more than 8 times, a bound that some block reaches.
All inputs are finite; a program needn't handle non-finite values.
Results may differ from a plain program's by a relative error of at most 0.035.
Values may be sent and summed in bfloat16 or wider, within the bound.
A program may use at most 64 MiB of HBM per device.

v0:
```python
import jax
import jax.numpy as jnp
from jax import lax
from jax.sharding import PartitionSpec as P

H = 16
C = 32
RC = 8


EPS_NORM = 1e-05
EPS_MEMORY = 1e-06
NEG_BIG = -1e30


def shifted(block, axis, distance):
    devices = range(lax.axis_size(axis))
    route = [(i - distance, i) for i in devices if i - distance in devices]
    return lax.ppermute(block, axis, route)


def layer_norm(values_in, gain):
    values_in = values_in.astype(jnp.float32)
    centre = jnp.mean(values_in, axis=-1, keepdims=True)
    centred = values_in - centre
    spread = jnp.mean(centred * centred, axis=-1, keepdims=True)
    return centred * lax.rsqrt(spread + EPS_NORM) * gain


def span_memory(normed, live_mask, gain, span_len):
    model_width = normed.shape[1]
    masked = jnp.where(live_mask[:, None], normed.astype(jnp.float32), jnp.float32(0.0))
    owner_sums = masked.reshape(-1, span_len, model_width).sum(axis=1)
    counts = live_mask.reshape(-1, span_len).astype(jnp.float32).sum(axis=1)
    means = owner_sums / jnp.maximum(counts, 1.0)[:, None]
    power = jnp.mean(means * means, axis=-1, keepdims=True)
    return (means * lax.rsqrt(power + EPS_MEMORY) * gain).astype(jnp.bfloat16)


def block_size():
    return 256


def local_part(query, keys, values, first_frame, length, head_count, span_len, right_len):
    frame_count, model_width = query.shape
    head_size = model_width // head_count
    group_rows = 4 * span_len
    group_count = frame_count // group_rows
    block_rows = block_size()
    query_blocks = query.reshape(group_count, group_rows, head_count, head_size)
    key_blocks = keys[:frame_count].reshape(group_count, group_rows, head_count, head_size)
    value_blocks = values[:frame_count].reshape(group_count, group_rows, head_count, head_size)
    key_tail = keys[frame_count:].reshape(1, right_len, head_count, head_size)
    value_tail = values[frame_count:].reshape(1, right_len, head_count, head_size)
    key_all = jnp.concatenate(
        [key_blocks, jnp.concatenate([key_blocks[1:, :right_len], key_tail], axis=0)], axis=1
    )
    value_all = jnp.concatenate(
        [value_blocks, jnp.concatenate([value_blocks[1:, :right_len], value_tail], axis=0)], axis=1
    )
    start_offsets = jnp.arange(group_count, dtype=jnp.int32)[:, None] * group_rows
    query_pos = first_frame + start_offsets + jnp.arange(group_rows, dtype=jnp.int32)[None, :]
    key_pos = first_frame + jnp.concatenate(
        [
            start_offsets + jnp.arange(group_rows, dtype=jnp.int32)[None, :],
            start_offsets + group_rows + jnp.arange(right_len, dtype=jnp.int32)[None, :],
        ],
        axis=1,
    )
    query_span = query_pos // span_len
    span_end = (query_span + 1) * span_len
    same = (key_pos // span_len)[:, None, :] == query_span[:, :, None]
    ahead = (key_pos[:, None, :] >= span_end[:, :, None]) & (
        key_pos[:, None, :] < span_end[:, :, None] + right_len
    )
    allowed = (same | ahead) & (key_pos < length)[:, None, :]
    scores = jnp.einsum(
        "gqhd,gkhd->ghqk", query_blocks, key_all, preferred_element_type=jnp.float32
    ) * head_size ** (-0.5)
    scores = jnp.where(allowed[:, None], scores, NEG_BIG)
    row_peak = jnp.max(scores, axis=-1)
    weights = jnp.where(allowed[:, None], jnp.exp(scores - row_peak[..., None]), jnp.float32(0.0))
    row_total = jnp.sum(weights, axis=-1)
    accum = jnp.einsum(
        "ghqk,gkhd->ghqd",
        weights.astype(jnp.bfloat16),
        value_all,
        preferred_element_type=jnp.float32,
    )
    block_count = frame_count // block_rows
    row_peak = (
        row_peak.transpose(1, 0, 2).reshape(head_count, block_count, block_rows).transpose(1, 0, 2)
    )
    row_total = (
        row_total.transpose(1, 0, 2).reshape(head_count, block_count, block_rows).transpose(1, 0, 2)
    )
    accum = (
        accum.transpose(1, 0, 2, 3)
        .reshape(head_count, block_count, block_rows, head_size)
        .transpose(1, 0, 2, 3)
    )
    return (row_peak, row_total, accum)


def memory_update(
    carry, memory_keys, memory_values, query, first_frame, length, head_count, span_len
):
    row_peak, row_total, accum = carry
    block_count, _, block_rows = row_peak.shape
    row_count, model_width = memory_keys.shape
    head_size = model_width // head_count
    mem_keys = memory_keys.reshape(row_count, head_count, head_size)
    mem_values = memory_values.reshape(row_count, head_count, head_size)
    mem_index = jnp.arange(row_count, dtype=jnp.int32)
    mem_live = mem_index * span_len < length
    query_blocks = query.reshape(block_count, block_rows, head_count, head_size)
    positions = first_frame + jnp.arange(block_count * block_rows, dtype=jnp.int32).reshape(
        block_count, block_rows
    )

    def one_block(packed):
        query_now, pos_now, peak_now, total_now, accum_now = packed
        scores = jnp.einsum(
            "qhd,khd->hqk", query_now, mem_keys, preferred_element_type=jnp.float32
        ) * head_size ** (-0.5)
        allowed = (mem_index[None, :] < (pos_now // span_len)[:, None]) & mem_live[None, :]
        scores = jnp.where(allowed[None], scores, NEG_BIG)
        new_peak = jnp.maximum(peak_now, jnp.max(scores, axis=-1))
        weights = jnp.where(allowed[None], jnp.exp(scores - new_peak[..., None]), jnp.float32(0.0))
        factor = jnp.exp(peak_now - new_peak)
        total_next = total_now * factor + jnp.sum(weights, axis=-1)
        accum_next = accum_now * factor[..., None] + jnp.einsum(
            "hqk,khd->hqd",
            weights.astype(jnp.bfloat16),
            mem_values,
            preferred_element_type=jnp.float32,
        )
        return (new_peak, total_next, accum_next)

    return lax.map(one_block, (query_blocks, positions, row_peak, row_total, accum))


def finish(carry, frame_count, model_width):
    row_peak, row_total, accum = carry
    result = accum / row_total[..., None]
    return result.transpose(0, 2, 1, 3).reshape(frame_count, model_width).astype(jnp.bfloat16)


def dispatch_matrix(owner_ids, owner_count, capacity):
    choose = (owner_ids[:, None] == jnp.arange(owner_count, dtype=jnp.int32)[None, :]).astype(
        jnp.int32
    )
    before = jnp.cumsum(choose, axis=0) - choose
    slot_index = jnp.sum(before * choose, axis=1)
    target = owner_ids * capacity + slot_index
    slot_rows = jnp.arange(owner_count * capacity, dtype=jnp.int32)
    return (slot_rows[:, None] == target[None, :]).astype(jnp.bfloat16)


def per_device(
    frames,
    lengths,
    norm_gain,
    memory_gain,
    qkv_weight,
    out_weight,
    segment_ids,
    owners,
    language_weight,
):
    local_frames = frames[0]
    frame_count, model_width = local_frames.shape
    head_count = H
    time_count = lax.axis_size("tm")
    first_frame = lax.axis_index("tm") * frame_count
    length = lengths[0]
    live_mask = first_frame + jnp.arange(frame_count, dtype=jnp.int32) < length
    right_frames = shifted(local_frames[:RC], "tm", -1)
    normed = layer_norm(local_frames, norm_gain).astype(jnp.bfloat16)
    normed_right = layer_norm(right_frames, norm_gain).astype(jnp.bfloat16)
    memory = span_memory(normed, live_mask, memory_gain, C)
    stacked_rows = jnp.concatenate([normed, normed_right, memory], axis=0)
    projected = jnp.einsum(
        "fd,kdw->kfw",
        stacked_rows,
        lax.all_gather(qkv_weight, "tm", axis=2, tiled=True),
        preferred_element_type=jnp.float32,
    ).astype(jnp.bfloat16)
    split_at = frame_count + RC
    query = projected[0, :frame_count]
    keys = projected[1, :split_at]
    values = projected[2, :split_at]
    memory_keys = projected[1, split_at:]
    memory_values = projected[2, split_at:]
    carry = local_part(query, keys, values, first_frame, length, head_count, C, RC)
    carry = memory_update(
        carry,
        lax.all_gather(memory_keys, "tm", axis=0, tiled=True),
        lax.all_gather(memory_values, "tm", axis=0, tiled=True),
        query,
        first_frame,
        length,
        head_count,
        C,
    )
    attended = finish(carry, frame_count, model_width)
    output_proj = jnp.dot(
        attended,
        lax.all_gather(out_weight, "tm", axis=1, tiled=True),
        preferred_element_type=jnp.float32,
    )
    encoded = jnp.where(
        live_mask[:, None], local_frames.astype(jnp.float32) + output_proj, jnp.float32(0.0)
    ).astype(jnp.bfloat16)
    token_count = owners.shape[2]
    segments = segment_ids[0, 0]
    owner_indicator = (
        segments[None, :] == jnp.arange(token_count, dtype=jnp.int32)[:, None]
    ).astype(jnp.bfloat16)
    owner_sums = jnp.dot(owner_indicator, encoded, preferred_element_type=jnp.float32)
    counts = jnp.sum(owner_indicator.astype(jnp.float32), axis=1)
    pooled_rows = (owner_sums / counts[:, None]).astype(jnp.bfloat16)
    slot_count = 2 * token_count
    capacity = slot_count // time_count
    route_matrix = dispatch_matrix(owners[0, 0, :, 0], time_count, capacity)
    sent_rows = jnp.dot(route_matrix, pooled_rows, preferred_element_type=jnp.float32).astype(
        jnp.bfloat16
    )
    received = lax.all_to_all(
        sent_rows.reshape(time_count, capacity, model_width),
        "tm",
        split_axis=0,
        concat_axis=0,
        tiled=True,
    )
    received = received.reshape(slot_count, model_width)
    lm_out = jnp.dot(
        received,
        lax.all_gather(language_weight, "rec", axis=1, tiled=True),
        preferred_element_type=jnp.float32,
    ).astype(jnp.bfloat16)
    return (encoded[None], lm_out[None, None])


def solution(mesh):
    in_specs = (
        P("rec", "tm", None),
        P("rec"),
        P(),
        P(),
        P(None, None, "tm"),
        P(None, "tm"),
        P("rec", "tm", None),
        P("rec", "tm", None, None),
        P(None, "rec"),
    )
    out_specs = (P("rec", "tm", None), P("rec", "tm", None, None))
    return jax.shard_map(
        per_device, mesh=mesh, in_specs=in_specs, out_specs=out_specs, check_vma=False
    )
```

profile of v0, /device:TPU:1, one launch (start us, length us, event | category | flops | bytes accessed | tf_op | source)
XLA Modules:
  0.0 387.2 jit_solution(15839129168917693151)
XLA Ops:
  7.2 0.7 all-gather.8.cloned.1.call-update
  8.0 0.7 slice_bitcast_fusion
  8.7 1.3 collective-permute-start
  10.6 1.4 convert_reduce_fusion
  12.2 1.6 multiply_reduce_fusion
  13.9 0.1 convert_reduce_fusion.3
  14.1 0.7 select_reduce_fusion
  14.8 0.2 multiply_reduce_fusion.1
  15.0 1.4 multiply_convert_fusion.1
  16.4 0.1 convert_reduce_fusion.2
  16.5 0.2 fusion.79
  16.8 85.9 %all-gather.8.cloned.1.call-done = bf16[3,1024,1024]{1,2,0:T(8,128)(2,1)} async-done(((bf16[3,1024,32]{1,2,0:T(8,128)(2,1)}), bf16[3,1024,1024]{1,2,0:T(8,128)(2,1)}) %all-gather.8.cloned.1.call-update) | async-done | bytes 6291472 | tf_op jit(solution)/shard_map/all_gather | solution.py:186
  102.8 6.7 %convert_bitcast_fusion = bf16[3,536,1024]{2,1,0:T(8,128)(2,1)S(1)} fusion(bf16[3,1024,1024]{1,2,0:T(8,128)(2,1)} %all-gather.8.cloned.1.call-done, bf16[16,1024]{1,0:T(8,128)(2,1)S(1)} %multiply_convert_fusion.2, bf16[8,1024]{1,0:T(8,128)(2,1)S(1)} %fusion.81, bf16[512,1024]{1,0:T(8,128)(2,1)} %multiply_convert_fusion.1), kind=kOutput, calls=%fused_computation.43 | convolution fusion | flops 3377160192 | bytes 10682368 | tf_op jit(solution)/shard_map/fd,kdw->kfw/dot_general | solution.py:183
  109.5 0.6 fusion.93
  110.2 0.7 all-gather.16.cloned.1.call-update
  111.0 0.5 all-gather.10.cloned.1.call-update
  111.6 0.5 all-gather.12.cloned.1.call-update
  112.6 0.2 reduce_window_sum.11
  112.8 0.2 select_reduce_fusion.1
  113.0 0.3 or_and_fusion
  113.3 3.5 fusion.94
  116.8 2.4 reshape.439
  119.2 1.3 reshape.440
  120.5 0.8 copy.85
  121.3 4.0 %reshape.441 = bf16[4,128,16,64]{3,2,1,0:T(8,128)(2,1)} reshape(bf16[1,512,1024]{2,1,0:T(8,128)(2,1)} %get-tuple-element.258) | data formatting | bytes 2097152 | tf_op jit(solution)/shard_map/reshape | solution.py:51
  125.3 2.8 copy.66
  128.2 3.1 fusion.33
  131.4 1.3 fusion.35
  132.7 0.7 copy-done.2
  133.5 2.5 copy.80
  136.0 0.9 copy.88
  136.9 1.3 reshape.442
  138.2 1.8 copy.75
  140.0 3.7 fusion.58
  143.7 2.8 copy.76
  146.4 3.1 reshape.429
  149.6 29.8 %all-gather.14.cloned.1.call-done = bf16[1,512,1024]{2,1,0:T(8,128)(2,1)} async-done(((bf16[1,16,1024]{2,1,0:T(8,128)(2,1)}), bf16[1,512,1024]{2,1,0:T(8,128)(2,1)}) %all-gather.14.cloned.1.call-update) | async-done | bytes 1048592 | tf_op jit(solution)/shard_map/all_gather | solution.py:198
  179.4 1.5 copy.71
  180.9 74.9 %all-gather.16.cloned.1.call-done = bf16[1,512,1024]{2,1,0:T(8,128)(2,1)} async-done(((bf16[1,16,1024]{2,1,0:T(8,128)(2,1)}), bf16[1,512,1024]{2,1,0:T(8,128)(2,1)}) %all-gather.16.cloned.1.call-update) | async-done | bytes 1048592 | tf_op jit(solution)/shard_map/all_gather | solution.py:199
  255.8 2.3 copy.77
  258.1 22.3 %while.15 = (s32[]{:T(128)}, f32[2,16,256]{2,1,0:T(8,128)S(1)}, f32[2,16,256,64]{2,3,1,0:T(8,128)}, f32[2,16,256]{2,0,1:T(2,128)S(1)}, f32[2,16,256]{2,0,1:T(2,1...) while((s32[]{:T(128)}, f32[2,16,256]{2,1,0:T(8,128)S(1)}, ...), condition=%wide.region_12.13_spmd.clone, body=%wide.region_9.12_spmd.clone.sunk | while | flops 564941568 | bytes 53778668 | solution.py:140
  258.1 0.7 multiply_compare_fusion.2
  258.8 0.2 fusion.115
  259.0 2.8 fusion.116
  261.8 2.6 fusion.118
  264.4 1.1 constant_dynamic-slice_fusion.9
  265.5 2.4 fusion.120
  267.9 1.3 copy-done.6
  269.3 0.7 multiply_compare_fusion.2
  270.0 0.2 fusion.115
  270.1 2.8 fusion.116
  273.0 2.6 fusion.118
  275.6 1.1 constant_dynamic-slice_fusion.9
  276.7 2.4 fusion.120
  279.1 1.3 copy-done.6
  280.4 1.8 fusion.69
  282.3 1.1 copy.82
  283.4 0.2 copy.96
  283.6 50.7 %all-gather.10.cloned.1.call-done = bf16[1024,1024]{0,1:T(8,128)(2,1)} async-done(((bf16[1024,32]{0,1:T(8,128)(2,1)}), bf16[1024,1024]{0,1:T(8,128)(2,1)}) %all-gather.10.cloned.1.call-update) | async-done | bytes 2097168 | tf_op jit(solution)/shard_map/all_gather | solution.py:209
  334.3 3.0 fusion.57
  337.4 1.3 fusion.63
  338.7 4.9 %all-to-all-start = ((bf16[32,8,1024]{2,1,0:T(8,128)(2,1)}), bf16[32,8,1024]{2,1,0:T(8,128)(2,1)S(1)}, u32[]{:S(2)}, u32[]{:S(2)}) async-start(bf16[32,8,1024]{2,1,0:T(8,128)(2,1)} %fusion.63), calls=%async_computation | async-start | bytes 1048576 | tf_op jit(solution)/shard_map/all_to_all | solution.py:229
  343.6 32.6 %all-gather.12.cloned.1.call-done = bf16[1024,2048]{1,0:T(8,128)(2,1)} async-done(((bf16[1024,256]{1,0:T(8,128)(2,1)}), bf16[1024,2048]{1,0:T(8,128)(2,1)}) %all-gather.12.cloned.1.call-update) | async-done | bytes 4194320 | tf_op jit(solution)/shard_map/all_gather | solution.py:239
  376.2 4.4 %fusion.36 = bf16[1,1,256,2048]{3,2,1,0:T(8,128)(2,1)} fusion(bf16[1024,2048]{1,0:T(8,128)(2,1)} %all-gather.12.cloned.1.call-done, bf16[32,8,1024]{2,1,0:T(8,128)(2,1)S(1)} %all-to-all-done), kind=kOutput, calls=%fused_computation.47 | convolution fusion | flops 1074266112 | bytes 5767168 | tf_op jit(solution)/shard_map/dot_general | solution.py:237
  (80 shorter events, 1.5 us)
Async XLA Ops:
  7.2 6.9 %copy-start = (bf16[1,512,1024]{2,1,0:T(8,128)(2,1)S(1)}, bf16[1,512,1024]{2,1,0:T(8,128)(2,1)}, u32[]{:S(2)}) copy-start(bf16[1,512,1024]{2,1,0:T(8,128)(2,1)} %param.11) | copy-start | bytes 3145732
  7.2 6.9 %copy-start.8 = (f32[1024]{0:T(1024)S(1)}, f32[1024]{0:T(1024)}, u32[]{:S(2)}) copy-start(f32[1024]{0:T(1024)} %param.13) | copy-start | bytes 12292
  7.2 95.6 %all-gather.8.cloned.1.call-start = ((), (), s32[]{:S(2)}) async-start(), calls=%async_computation.1 | async-start | bytes 6488064 | tf_op jit(solution)/shard_map/all_gather | solution.py:186
  7.9 171.5 %all-gather.14.cloned.1.call-start = ((), (), s32[]{:S(2)}) async-start(), calls=%async_computation.4 | async-start | bytes 1081344 | tf_op jit(solution)/shard_map/all_gather | solution.py:198
  8.7 7.7 %collective-permute-start = (bf16[8,1024]{1,0:T(8,128)(2,1)S(1)}, bf16[8,1024]{1,0:T(8,128)(2,1)S(1)}, u32[]{:S(2)}, u32[]{:S(2)}) collective-permute-start(bf16[8,1024]{1,0:T(8,128)(2,1)S(1)} %slice_bitcast_fusion), channel_id=1, source_target_pairs={{1,0},{2,1},{3,2},{4,3},{5,4},{6,5},{7,6},{8,7},{9,8},{10,9},{11,1... | collective-permute-start | bytes 49160 | tf_op jit(solution)/shard_map/ppermute | solution.py:19
  12.1 4.3 %copy-start.9 = (f32[1024]{0:T(1024)S(1)}, f32[1024]{0:T(1024)}, u32[]{:S(2)}) copy-start(f32[1024]{0:T(1024)} %param.14) | copy-start | bytes 12292
  16.8 95.6 %copy-start.11 = (s32[1,1,512]{2,1,0:T(1,128)S(1)}, s32[1,1,512]{2,1,0:T(1,128)}, u32[]{:S(2)}) copy-start(s32[1,1,512]{2,1,0:T(1,128)} %param.17) | copy-start | bytes 6148
  16.8 95.7 %copy-start.10 = (s32[1,1,128,1]{2,3,1,0:T(1,128)S(1)}, s32[1,1,128,1]{2,3,1,0:T(1,128)}, u32[]{:S(2)}) copy-start(s32[1,1,128,1]{2,3,1,0:T(1,128)} %param.18) | copy-start | bytes 1540
  109.5 3.8 copy-start.4
  110.2 145.6 %all-gather.16.cloned.1.call-start = ((), (), s32[]{:S(2)}) async-start(), calls=%async_computation.5 | async-start | bytes 1081344 | tf_op jit(solution)/shard_map/all_gather | solution.py:199
  110.9 223.4 %all-gather.10.cloned.1.call-start = ((), (), s32[]{:S(2)}) async-start(), calls=%async_computation.2 | async-start | bytes 2162688 | tf_op jit(solution)/shard_map/all_gather | solution.py:209
  111.5 264.7 %all-gather.12.cloned.1.call-start = ((), (), s32[]{:S(2)}) async-start(), calls=%async_computation.3 | async-start | bytes 4718592 | tf_op jit(solution)/shard_map/all_gather | solution.py:239
  131.4 2.0 copy-start.2
  133.4 3.5 copy-start.3
  261.8 3.7 copy-start.5
  261.8 3.7 copy-start.7
  267.9 1.3 copy-start.6
  272.9 3.7 copy-start.5
  273.0 3.7 copy-start.7
  279.1 1.3 copy-start.6
  282.3 52.1 %copy-start.1 = (bf16[1,512,1024]{2,1,0:T(8,128)(2,1)S(1)}, bf16[1,512,1024]{2,1,0:T(8,128)(2,1)}, u32[]{:S(2)}) copy-start(bf16[1,512,1024]{2,1,0:T(8,128)(2,1)} %param.11) | copy-start | bytes 3145732
  337.3 43.3 %copy-start.12 = (bf16[512,1024]{1,0:T(8,128)(2,1)}, bf16[512,1024]{1,0:T(8,128)(2,1)S(1)}, u32[]{:S(2)}) copy-start(bf16[512,1024]{1,0:T(8,128)(2,1)S(1)} %fusion.57) | copy-start | bytes 3145732
  338.7 37.5 %all-to-all-start = ((bf16[32,8,1024]{2,1,0:T(8,128)(2,1)}), bf16[32,8,1024]{2,1,0:T(8,128)(2,1)S(1)}, u32[]{:S(2)}, u32[]{:S(2)}) async-start(bf16[32,8,1024]{2,1,0:T(8,128)(2,1)} %fusion.63), calls=%async_computation | async-start | bytes 1048576 | tf_op jit(solution)/shard_map/all_to_all | solution.py:229
Sparse Core Ops, SparseCore 0:
  10.6 92.1 all-gather.7
  110.3 69.0 all-gather.13
  182.0 73.7 all-gather.15
  258.3 76.0 all-gather.9
  336.0 40.1 all-gather.11
where the time goes:
time: 388 us; the launch traced here: 387 us
  waiting for transfers between devices  276 us (71%)
  local copies, waits for them, and re-layouts  39.7 us (10%)
  matrix products  32.6 us (8%)
  other arithmetic  17.1 us (4%)
  between operations  14.8 us (4%)
  starting transfers between devices  6.39 us (2%)
    all_gather x1, waiting for transfers between devices, per_device(): lax.all_gather(qkv_weight, 'tm', axis=2, tiled=True)  85.9 us
    all_gather x1, waiting for transfers between devices, per_device(): lax.all_gather(memory_values, 'tm', axis=0, tiled=True)  74.9 us
    all_gather x1, waiting for transfers between devices, per_device(): lax.all_gather(out_weight, 'tm', axis=1, tiled=True)  50.7 us
    all_gather x1, waiting for transfers between devices, per_device(): lax.all_gather(language_weight, 'rec', axis=1, tiled=True)  32.6 us
    all_gather x1, waiting for transfers between devices, per_device(): lax.all_gather(memory_keys, 'tm', axis=0, tiled=True)  29.8 us
  transfers between devices with their start and end apart: 7, of which 5 were waited for; matrix products, arithmetic and copies ran while one was open for 19% of the time, Pallas kernels for 0%

commit v1 on v0

v1 whole, which is shorter than its diff:
```python
import functools

import jax
import jax.numpy as jnp
from jax import lax
from jax.experimental import pallas as pl
from jax.experimental.pallas import tpu as pltpu
from jax.sharding import PartitionSpec as P

H = 16
C = 32
RC = 8
EPS_NORM = 1e-05
EPS_MEMORY = 1e-06
NEG_BIG = -1e30

NX, NZ, NY = 4, 8, 4
N_TM = NX * NZ
F = 512
D = 1024
DL = 2048
TOK = 128
CAP = 8
SLOTS = 256
G = 4
GW = D // G
QB = 128
MEM = N_TM * F // C
KW = MEM + 2 * QB
BF = jnp.bfloat16
F32 = jnp.float32


def dot_nt(a, b):
    return lax.dot_general(a, b, (((1,), (1,)), ((), ())), preferred_element_type=F32)


def dot_nn(a, b):
    return lax.dot_general(a, b, (((1,), (0,)), ((), ())), preferred_element_type=F32)


def wrap(a, n):
    return lax.rem(a + 2 * n, n)


def kernel(
    frames, lengths, norm_gain, memory_gain, wq_hbm, wo_hbm, segments, owners, lw_hbm,
    enc_hbm, lm_hbm,
    wg, owg, lwg, xs, mg, mrows, q4, kk, vv, att, bias, ri, cnt, enc, sb, rb, lmo,
    w_send, w_recv, m_send, m_recv, o_send, o_recv, ws_send, ws_recv, os_send, os_recv,
    r_send, r_recv, l_send, l_recv, ls_send, ls_recv, a_send, a_recv, own_sem, out_sem,
):
    r = lax.axis_index("rec")
    t = lax.axis_index("tm")
    y, c = r // 2, lax.rem(r, 2)
    x, z = t // NZ, lax.rem(t, NZ)
    sib = (y * 2 + (1 - c), t)
    first_frame = t * F
    length = lengths[0]

    barrier = pltpu.get_barrier_semaphore()

    @pl.loop(1, N_TM)
    def _(d):
        pl.semaphore_signal(
            barrier, inc=1, device_id=(r, lax.rem(t + d, N_TM)), device_id_type=pl.DeviceIdType.MESH
        )

    @pl.loop(1, 2 * NY)
    def _(d):
        pl.semaphore_signal(
            barrier, inc=1, device_id=(lax.rem(r + d, 2 * NY), t), device_id_type=pl.DeviceIdType.MESH
        )

    pl.semaphore_wait(barrier, N_TM - 1 + 2 * NY - 1)

    def remote(src, dst, send, recv, device):
        return pltpu.make_async_remote_copy(
            src_ref=src,
            dst_ref=dst,
            send_sem=send,
            recv_sem=recv,
            device_id=device,
            device_id_type=pl.DeviceIdType.MESH,
        )

    steps = {
        0: [("z", k) for k in range(1, NZ // 2 + 1)] + [("x", k) for k in range(1, NX // 2 + 1)],
        1: [("x", k) for k in range(1, NX // 2 + 1)] + [("z", k) for k in range(1, NZ // 2 + 1)],
    }
    n_steps = len(steps[0])

    def size_pos(axis):
        return (NZ, z) if axis == "z" else (NX, x)

    def neighbour(axis, by):
        if axis == "z":
            return (r, x * NZ + wrap(z + by, NZ))
        return (r, wrap(x + by, NX) * NZ + z)

    def w_piece(v, axis, o):
        if v == 0:
            return wg.at[:, x, o, 0] if axis == "z" else wg.at[:, o, :, 0]
        return wg.at[:, o, z, 1] if axis == "x" else wg.at[:, :, o, 1]

    def o_piece(v, axis, o):
        if v == 0:
            return owg.at[x, o, 0] if axis == "z" else owg.at[o, :, 0]
        return owg.at[o, z, 1] if axis == "x" else owg.at[:, o, 1]

    def m_piece(v, axis, o):
        if v == 0:
            return mg.at[x, o] if axis == "z" else mg.at[o]
        return mg.at[o, z] if axis == "x" else mg.at[:, o]

    def cut(ref, axis, k, d):
        n = NZ if axis == "z" else NX
        if k < n // 2:
            return ref
        where = (slice(None),) * (len(ref.shape) - 1)
        return ref.at[where + (pl.ds(d * (D // 2), D // 2),)]

    def ring_start(v, i, piece, send, recv, own=None):
        axis, k = steps[v][i]
        n, pos = size_pos(axis)
        for d, s in enumerate((1, -1)):
            dst = cut(piece(v, axis, wrap(pos - s * (k - 1), n)), axis, k, d)
            src = own if own is not None and i == 0 else dst
            remote(src, dst, send.at[2 * i + d], recv.at[2 * i + d], neighbour(axis, s)).start()

    def ring_in(v, i, piece):
        axis, k = steps[v][i]
        n, pos = size_pos(axis)
        return [cut(piece(v, axis, wrap(pos - s * k, n)), axis, k, d) for d, s in enumerate((1, -1))]

    def ring_wait(v, i, piece, send, recv):
        axis, _ = steps[v][i]
        for d, ref in enumerate(ring_in(v, i, piece)):
            copy = remote(ref, ref, send.at[2 * i + d], recv.at[2 * i + d], neighbour(axis, 1))
            copy.wait_recv()
            copy.wait_send()

    def sib_start(v, i, piece, send, recv):
        for d, ref in enumerate(ring_in(v, i, piece)):
            remote(ref, ref, send.at[2 * i + d], recv.at[2 * i + d], sib).start()

    def sib_wait(v, i, piece, send, recv):
        for d, ref in enumerate(ring_in(v, i, piece)):
            remote(ref, ref, send.at[2 * i + d], recv.at[2 * i + d], sib).wait_send()
        for d, ref in enumerate(ring_in(1 - v, i, piece)):
            remote(ref, ref, send.at[2 * i + d], recv.at[2 * i + d], sib).wait_recv()

    def per_core(fn):
        for v in (0, 1):
            pl.when(c == v)(functools.partial(fn, v))

    own_copies = []
    for v in (0, 1):
        own_copies.append(
            pltpu.make_async_copy(wq_hbm.at[:, pl.ds(16 * v, 16)], wg.at[:, x, z, v], own_sem.at[v])
        )
        own_copies.append(
            pltpu.make_async_copy(wo_hbm.at[pl.ds(16 * v, 16)], owg.at[x, z, v], own_sem.at[2 + v])
        )
    own_copies.append(pltpu.make_async_copy(lw_hbm, lwg.at[r], own_sem.at[4]))

    def first_hop(v):
        ring_start(v, 0, w_piece, w_send, w_recv, own=wq_hbm.at[:, pl.ds(16 * v, 16)])

    per_core(first_hop)
    for copy in own_copies:
        copy.start()

    gain = norm_gain[...]

    @pl.loop(0, F // C)
    def _(i):
        rows = pl.ds(pl.multiple_of(i * C, C), C)
        v = frames[rows, :].astype(F32)
        centred = v - jnp.mean(v, axis=1, keepdims=True)
        spread = jnp.mean(centred * centred, axis=1, keepdims=True)
        normed = (centred * lax.rsqrt(spread + EPS_NORM) * gain).astype(BF)
        xs[rows, :] = normed
        start = first_frame + i * C
        live = start + lax.broadcasted_iota(jnp.int32, (C, 1), 0) < length
        total = jnp.sum(jnp.where(live, normed.astype(F32), 0.0), axis=0, keepdims=True)
        count = jnp.clip(length - start, 1, C).astype(F32)
        mrows[pl.ds(i, 1), :] = total / count

    means = mrows[...]
    power = jnp.mean(means * means, axis=1, keepdims=True)
    mg[x, z] = (means * lax.rsqrt(power + EPS_MEMORY) * memory_gain[...]).astype(BF)

    right = remote(
        xs.at[pl.ds(0, 16)], xs.at[pl.ds(F, 16)], r_send.at[0], r_recv.at[0], (r, wrap(t - 1, N_TM))
    )
    right.start()
    for copy in own_copies:
        copy.wait()

    def memory_hop(v):
        ring_start(v, 0, m_piece, m_send, m_recv)

    per_core(memory_hop)

    lw_up, lw_down = wrap(y + 1, NY), wrap(y - 1, NY)
    lw_far = wrap(y + 2, NY)

    def lw_half(slot, d):
        return lwg.at[slot, pl.ds(d * (D // 2), D // 2)]

    lw_first = [
        remote(lwg.at[r], lwg.at[r], l_send.at[0], l_recv.at[0], (lw_up * 2 + c, t)),
        remote(lwg.at[r], lwg.at[r], l_send.at[1], l_recv.at[1], (lw_down * 2 + c, t)),
        remote(lwg.at[r], lwg.at[r], ls_send.at[0], ls_recv.at[0], sib),
    ]

    span0 = t * (F // C)

    @pl.loop(0, F // QB)
    def _(b):
        q = b * QB + lax.broadcasted_iota(jnp.int32, (QB, KW), 0)
        n = lax.broadcasted_iota(jnp.int32, (QB, KW), 1)
        q_span = q // C
        u = b * QB + n - MEM
        in_memory = (n < MEM) & (n < span0 + q_span) & (n * C < length)
        same = (u // C) == q_span
        ahead = (u >= (q_span + 1) * C) & (u < (q_span + 1) * C + RC)
        in_frames = (n >= MEM) & (same | ahead) & (first_frame + u < length)
        bias[b] = jnp.where(in_memory | in_frames, 0.0, NEG_BIG)

    own_row = jnp.broadcast_to(owners[...].astype(F32), (TOK, TOK))
    own_col = own_row.T
    earlier = lax.broadcasted_iota(jnp.int32, (TOK, TOK), 0) < lax.broadcasted_iota(
        jnp.int32, (TOK, TOK), 1
    )
    slot = jnp.sum(jnp.where((own_row == own_col) & earlier, 1.0, 0.0), axis=0, keepdims=True)
    target = owners[...].astype(F32) * CAP + slot
    place = lax.broadcasted_iota(jnp.int32, (SLOTS, TOK), 0).astype(F32)
    route = jnp.where(place == target, 1.0, 0.0).astype(BF)
    member = jnp.where(
        lax.broadcasted_iota(jnp.int32, (TOK, F), 0) == segments[...], 1.0, 0.0
    ).astype(BF)
    chosen = dot_nn(route, member)
    ri[...] = chosen.astype(BF)
    cnt[...] = jnp.broadcast_to(
        jnp.maximum(jnp.sum(chosen, axis=1, keepdims=True), 1.0), (SLOTS, 128)
    )

    def gather(v):
        for i in range(n_steps):
            ring_wait(v, i, w_piece, w_send, w_recv)
            if i + 1 < n_steps:
                ring_start(v, i + 1, w_piece, w_send, w_recv)
            sib_start(v, i, w_piece, ws_send, ws_recv)
            ring_wait(v, i, m_piece, m_send, m_recv)
            if i + 1 < n_steps:
                ring_start(v, i + 1, m_piece, m_send, m_recv)
        ring_start(v, 0, o_piece, o_send, o_recv)
        for i in range(n_steps):
            sib_wait(v, i, w_piece, ws_send, ws_recv)

    per_core(gather)
    for copy in lw_first:
        copy.start()
    right.wait()

    kk[pl.ds(MEM + F, QB), :] = jnp.zeros((QB, GW), BF)
    vv[pl.ds(MEM + F, QB), :] = jnp.zeros((QB, GW), BF)
    lane_head = lax.broadcasted_iota(jnp.int32, (1, GW), 1) // (D // H)

    def out_step(v, i):
        ring_wait(v, i, o_piece, o_send, o_recv)
        if i + 1 < n_steps:
            ring_start(v, i + 1, o_piece, o_send, o_recv)
        sib_start(v, i, o_piece, os_send, os_recv)

    lw_second = [
        remote(lw_half(lw_down * 2 + c, 0), lw_half(lw_down * 2 + c, 0), l_send.at[2], l_recv.at[2], (lw_up * 2 + c, t)),
        remote(lw_half(lw_up * 2 + c, 1), lw_half(lw_up * 2 + c, 1), l_send.at[3], l_recv.at[3], (lw_down * 2 + c, t)),
        remote(lwg.at[lw_down * 2 + c], lwg.at[lw_down * 2 + c], ls_send.at[1], ls_recv.at[1], sib),
        remote(lwg.at[lw_up * 2 + c], lwg.at[lw_up * 2 + c], ls_send.at[2], ls_recv.at[2], sib),
    ]
    lw_third = remote(lwg.at[lw_far * 2 + c], lwg.at[lw_far * 2 + c], ls_send.at[3], ls_recv.at[3], sib)

    def hop(slot_ref, k):
        return remote(slot_ref, slot_ref, l_send.at[k], l_recv.at[k], sib)

    def side(slot_ref, k):
        return remote(slot_ref, slot_ref, ls_send.at[k], ls_recv.at[k], sib)

    def lw_step_two():
        hop(lwg.at[lw_down * 2 + c], 0).wait_recv()
        hop(lwg.at[lw_up * 2 + c], 1).wait_recv()
        for copy in lw_second:
            copy.start()

    def lw_step_three():
        hop(lw_half(lw_far * 2 + c, 0), 2).wait_recv()
        hop(lw_half(lw_far * 2 + c, 1), 3).wait_recv()
        lw_third.start()

    @pl.loop(0, G)
    def _(j):
        g = wrap(x + j, NX)

        @pl.loop(0, 2)
        def _(i):
            rows = pl.ds(pl.multiple_of(i * 256, 256), 256)
            a = xs[rows, :]
            q = dot_nt(a, wg[0, g].reshape(GW, D)) * (D // H) ** -0.5
            for h in range(4):
                q4[h, rows, :] = jnp.where(lane_head == h, q, 0.0).astype(BF)
            at = pl.ds(pl.multiple_of(MEM + i * 256, 256), 256)
            kk[at, :] = dot_nt(a, wg[1, g].reshape(GW, D)).astype(BF)
            vv[at, :] = dot_nt(a, wg[2, g].reshape(GW, D)).astype(BF)
            a = mg[pl.ds(2 * i, 2)].reshape(256, D)
            kk[rows, :] = dot_nt(a, wg[1, g].reshape(GW, D)).astype(BF)
            vv[rows, :] = dot_nt(a, wg[2, g].reshape(GW, D)).astype(BF)

        a = xs[pl.ds(F, 16), :]
        kk[pl.ds(MEM + F, 16), :] = dot_nt(a, wg[1, g].reshape(GW, D)).astype(BF)
        vv[pl.ds(MEM + F, 16), :] = dot_nt(a, wg[2, g].reshape(GW, D)).astype(BF)

        for jj in range(G):

            @pl.when(j == jj)
            def _():
                def one(v):
                    if jj < 3:
                        out_step(v, 2 * jj)

                per_core(one)
                if jj == 2:
                    lw_step_two()

        @pl.loop(0, F // QB)
        def _(b):
            rows = pl.ds(pl.multiple_of(b * QB, QB), QB)
            near = pl.ds(pl.multiple_of(MEM + b * QB, QB), 2 * QB)
            q = q4[:, rows, :].reshape(4 * QB, GW)
            far_keys, near_keys = kk[pl.ds(0, MEM), :], kk[near, :]
            s = jnp.concatenate([dot_nt(q, far_keys), dot_nt(q, near_keys)], axis=1)
            s = (s.reshape(4, QB, KW) + bias[b][None]).reshape(4 * QB, KW)
            peak = jnp.max(s, axis=1, keepdims=True)
            w = jnp.exp(s - peak)
            total = jnp.sum(w, axis=1, keepdims=True)
            w = w.astype(BF)
            o = dot_nn(w[:, :MEM], vv[pl.ds(0, MEM), :]) + dot_nn(w[:, MEM:], vv[near, :])
            o = (o / total).reshape(4, QB, GW)
            out = o[3]
            for h in range(3):
                out = jnp.where(lane_head == h, o[h], out)
            att[g, rows, :] = out.astype(BF)

        for jj in range(G):

            @pl.when(j == jj)
            def _():
                def two(v):
                    if jj < 3:
                        out_step(v, 2 * jj + 1)

                per_core(two)
                if jj == 3:
                    lw_step_three()

    def out_end(v):
        for i in range(n_steps):
            sib_wait(v, i, o_piece, os_send, os_recv)

    per_core(out_end)

    @pl.loop(0, F // QB)
    def _(b):
        rows = pl.ds(pl.multiple_of(b * QB, QB), QB)
        w = owg[...].reshape(D, D)
        o = dot_nt(att[0, rows, :], w[:, :GW])
        for g in range(1, G):
            o += dot_nt(att[g, rows, :], w[:, g * GW : (g + 1) * GW])
        live = first_frame + b * QB + lax.broadcasted_iota(jnp.int32, (QB, 1), 0) < length
        enc[rows, :] = jnp.where(live, frames[rows, :].astype(F32) + o, 0.0).astype(BF)

    enc_out = pltpu.make_async_copy(enc, enc_hbm, out_sem.at[0])
    enc_out.start()

    sent = dot_nn(ri[...], enc[...]) / cnt[:, :1]
    sb[...] = sent.reshape(N_TM, CAP, D).astype(BF)
    rb[t] = sb[t]

    @pl.loop(1, N_TM)
    def _(d):
        to = lax.rem(t + d, N_TM)
        remote(sb.at[to], rb.at[t], a_send.at[d], a_recv.at[d], (r, to)).start()

    side(lwg.at[r], 0).wait_send()
    for k, slot in enumerate((r, lw_down * 2 + c, lw_up * 2 + c, lw_far * 2 + c)):
        if k:
            side(lwg.at[slot], k).wait_send()
        other = lax.rem(slot, 2)
        side(lwg.at[slot + 1 - 2 * other], k).wait_recv()
    hop(lwg.at[r], 0).wait_send()
    hop(lwg.at[r], 1).wait_send()
    hop(lw_half(r, 0), 2).wait_send()
    hop(lw_half(r, 0), 3).wait_send()

    @pl.loop(1, N_TM)
    def _(d):
        to = lax.rem(t + d, N_TM)
        source = wrap(t - d, N_TM)
        copy = remote(sb.at[to], rb.at[source], a_send.at[d], a_recv.at[d], (r, to))
        copy.wait_recv()
        copy.wait_send()

    got = rb[...].astype(F32).reshape(SLOTS, D).astype(BF)
    for k in range(2 * NY):
        lmo[:, k * 256 : (k + 1) * 256] = dot_nn(got, lwg[k]).astype(BF)
    lm_out = pltpu.make_async_copy(lmo, lm_hbm, out_sem.at[1])
    lm_out.start()
    enc_out.wait()
    lm_out.wait()


def per_device(
    frames, lengths, norm_gain, memory_gain, qkv_weight, out_weight, segment_ids, owners, language_weight
):
    vmem = pl.BlockSpec(memory_space=pltpu.VMEM)
    smem = pl.BlockSpec(memory_space=pltpu.SMEM)
    hbm = pl.BlockSpec(memory_space=pl.ANY)
    dma = pltpu.SemaphoreType.DMA
    n = 12
    enc, lm = pl.pallas_call(
        kernel,
        out_shape=(
            jax.ShapeDtypeStruct((F, D), BF),
            jax.ShapeDtypeStruct((SLOTS, DL), BF),
        ),
        in_specs=[vmem, smem, vmem, vmem, hbm, hbm, vmem, vmem, hbm],
        out_specs=(hbm, hbm),
        scratch_shapes=[
            pltpu.VMEM((3, NX, NZ, 2, 16, D), BF),
            pltpu.VMEM((NX, NZ, 2, 16, D), BF),
            pltpu.VMEM((2 * NY, D, DL // (2 * NY)), BF),
            pltpu.VMEM((F + 16, D), BF),
            pltpu.VMEM((NX, NZ, 16, D), BF),
            pltpu.VMEM((F // C, D), F32),
            pltpu.VMEM((4, F, GW), BF),
            pltpu.VMEM((MEM + F + QB, GW), BF),
            pltpu.VMEM((MEM + F + QB, GW), BF),
            pltpu.VMEM((G, F, GW), BF),
            pltpu.VMEM((F // QB, QB, KW), F32),
            pltpu.VMEM((SLOTS, F), BF),
            pltpu.VMEM((SLOTS, 128), F32),
            pltpu.VMEM((F, D), BF),
            pltpu.VMEM((N_TM, CAP, D), BF),
            pltpu.VMEM((N_TM, CAP, D), BF),
            pltpu.VMEM((SLOTS, DL), BF),
            dma((n,)), dma((n,)), dma((n,)), dma((n,)), dma((n,)), dma((n,)),
            dma((n,)), dma((n,)), dma((n,)), dma((n,)),
            dma((1,)), dma((1,)), dma((4,)), dma((4,)), dma((4,)), dma((4,)),
            dma((N_TM,)), dma((N_TM,)), dma((5,)), dma((2,)),
        ],
        compiler_params=pltpu.CompilerParams(
            collective_id=0, has_side_effects=True, vmem_limit_bytes=58 * 2**20
        ),
        name="block",
    )(
        frames[0],
        lengths,
        norm_gain[None],
        memory_gain[None],
        qkv_weight.transpose(0, 2, 1),
        out_weight.T,
        segment_ids[0],
        owners[0, :, :, 0],
        language_weight,
    )
    return (enc[None], lm[None, None])


def solution(mesh):
    in_specs = (
        P("rec", "tm", None),
        P("rec"),
        P(),
        P(),
        P(None, None, "tm"),
        P(None, "tm"),
        P("rec", "tm", None),
        P("rec", "tm", None, None),
        P(None, "rec"),
    )
    out_specs = (P("rec", "tm", None), P("rec", "tm", None, None))
    return jax.shard_map(
        per_device, mesh=mesh, in_specs=in_specs, out_specs=out_specs, check_vma=False
    )
```

time: 388 us -> 110 us (0.28)
  waiting for transfers between devices: 276 us -> 0 us
  Pallas kernels: 0 us -> 103 us
  local copies, waits for them, and re-layouts: 39.7 us -> 3.32 us
  matrix products: 32.6 us -> 0 us
  other arithmetic: 17.1 us -> 0 us
  between operations: 14.8 us -> 1.29 us
  starting transfers between devices: 6.39 us -> 0 us
    all_gather x5 -> x0, waiting for transfers between devices: 274 us -> none  [the longest x1 85.9 us: per_device(): lax.all_gather(qkv_weight, 'tm', axis=2, tiled=True)]
    pallas_call x0 -> x1, Pallas kernels: none -> 103 us  [per_device(): pl.pallas_call(kernel, out_shape=(jax.ShapeDtypeStruct((F, D), BF), jax.S...]
    dot_general x10 -> x0, matrix products: 32.6 us -> none  [the longest x1 6.73 us: per_device(): jnp.einsum('fd,kdw->kfw', stacked_rows, lax.all_gather(qkv_weight, 'tm',...]
    reshape x9 -> x0, local copies, waits for them, and re-layouts: 14.8 us -> none  [the longest x2 6.87 us: local_part(): keys[:frame_count].reshape(group_count, group_rows, head_count, head_size)]
    reduce_sum x12 -> x0, other arithmetic: 11.1 us -> none  [the longest x2 5.14 us: one_block(): total_next = total_now * factor + jnp.sum(weights, axis=-1)]
    slice x6 -> x0, local copies, waits for them, and re-layouts: 4.96 us -> none  [the longest x1 3.48 us: local_part(): values[:frame_count].reshape(group_count, group_rows, head_count, head_size)]
    all_to_all x1 -> x0, starting transfers between devices: 4.92 us -> none  [per_device(): lax.all_to_all(sent_rows.reshape(time_count, capacity, model_width), 'tm'...]
  transfers between devices with their start and end apart: 7 -> 0, of which waited for: 5 -> 0; matrix products, arithmetic and copies ran while one was open for 19% -> 0% of each run, Pallas kernels for 0% -> 0%
where the time goes in v1:
time: 110 us; the launch traced here: 108 us
  Pallas kernels  103 us (94%)
  local copies, waits for them, and re-layouts  3.32 us (3%)
  between operations  1.29 us (1%)
    pallas_call x1, Pallas kernels, per_device(): pl.pallas_call(kernel, out_shape=(jax.ShapeDtypeStruct((F, D), BF), jax.S...  103 us
    unnamed x4, local copies, waits for them, and re-layouts  3.32 us

profile of v1, /device:TPU:1, one launch (start us, length us, event | category | flops | bytes accessed | tf_op | source)
XLA Modules:
  0.0 108.0 jit_solution(11222400056569703761)
XLA Ops:
  1.3 103.4 %block.1 = (bf16[512,1024]{1,0:T(8,128)(2,1)}, bf16[256,2048]{1,0:T(8,128)(2,1)}) custom-call(bf16[512,1024]{1,0:T(8,128)(2,1)} %bitcast.9, s32[1]{0:T(128)S(6)} %copy.13.lengths, f32[1,1024]{1,0:T(1,128)} %bitcast.14, f32[1,1024]{1,0:T(1,128)} %bitcast.15, bf16[3,32,1024]{2,1,0:T(8,128)(2,1)} %bitcast.12, bf16[32,1024]{1,0:T(8,128)(2,1)} %bitcast.13, ...), custom_call_target="tpu_custom_call" | custom-call | tf_op jit(solution)/shard_map/block/pallas_call | solution.py:432
  104.7 0.0 copy-start
  104.7 2.4 %copy.14 = bf16[1,512,1024]{2,1,0:T(8,128)(2,1)} copy(bf16[1,512,1024]{2,1,0:T(8,128)(2,1)} %bitcast.11) | data formatting | bytes 2097152
  107.0 0.0 copy-done
  107.0 1.0 copy.15
Async XLA Ops:
  104.7 2.4 %copy-start = (bf16[256,2048]{1,0:T(8,128)(2,1)S(1)}, bf16[256,2048]{1,0:T(8,128)(2,1)}, u32[]{:S(2)}) copy-start(bf16[256,2048]{1,0:T(8,128)(2,1)} %get-tuple-element.5) | copy-start | bytes 3145732

commit v2 on v1

v2 whole, which is shorter than its diff:
```python
import functools

import jax
import jax.numpy as jnp
from jax import lax
from jax.experimental import pallas as pl
from jax.experimental.pallas import tpu as pltpu
from jax.sharding import PartitionSpec as P

H = 16
C = 32
RC = 8
EPS_NORM = 1e-05
EPS_MEMORY = 1e-06
NEG_BIG = -1e30

NX, NZ, NY = 4, 8, 4
N_TM = NX * NZ
F = 512
D = 1024
DL = 2048
TOK = 128
CAP = 8
SLOTS = 256
G = 4
GW = D // G
HEAD = D // H
QB = 64
MEM = N_TM * F // C
KW = MEM + 2 * QB
NCH = 2
CH = D // NCH
LOG2E = 1.4426950408889634
BF = jnp.bfloat16
F32 = jnp.float32


def dot_nt(a, b):
    return lax.dot_general(a, b, (((1,), (1,)), ((), ())), preferred_element_type=F32)


def dot_nn(a, b):
    return lax.dot_general(a, b, (((1,), (0,)), ((), ())), preferred_element_type=F32)


def wrap(a, n):
    return lax.rem(a + 2 * n, n)


def kernel(
    frames, lengths, norm_gain, memory_gain, wq_hbm, wo_hbm, segments, owners, lw_hbm,
    enc_hbm, lm_hbm,
    wg, owg, lwg, xs, mg, mrows, q4, kk, vv, att, bias, ri, cnt, enc, sb, rb, lacc, lmo,
    zw_send, zw_recv, zm_send, zm_recv, xw_send, xw_recv, xm_send, xm_recv, sw_send, sw_recv,
    oz_send, oz_recv, ox_send, ox_recv, oy_send, oy_recv, os_send, os_recv,
    r_send, r_recv, l_send, l_recv, ls_send, ls_recv, a_send, a_recv, own_sem, out_sem,
):
    r = lax.axis_index("rec")
    t = lax.axis_index("tm")
    y, c = r // 2, lax.rem(r, 2)
    x, z = t // NZ, lax.rem(t, NZ)
    sib = (y * 2 + (1 - c), t)
    first_frame = t * F
    length = lengths[0]

    barrier = pltpu.get_barrier_semaphore()

    @pl.loop(1, N_TM)
    def _(d):
        pl.semaphore_signal(
            barrier, inc=1, device_id=(r, lax.rem(t + d, N_TM)), device_id_type=pl.DeviceIdType.MESH
        )

    @pl.loop(1, 2 * NY)
    def _(d):
        pl.semaphore_signal(
            barrier, inc=1, device_id=(lax.rem(r + d, 2 * NY), t), device_id_type=pl.DeviceIdType.MESH
        )

    pl.semaphore_wait(barrier, N_TM - 1 + 2 * NY - 1)

    def remote(src, dst, send, recv, device):
        return pltpu.make_async_remote_copy(
            src_ref=src,
            dst_ref=dst,
            send_sem=send,
            recv_sem=recv,
            device_id=device,
            device_id_type=pl.DeviceIdType.MESH,
        )

    def at_z(by):
        return (r, x * NZ + wrap(z + by, NZ))

    def at_x(by):
        return (r, wrap(x + by, NX) * NZ + z)

    def at_y(by):
        return (wrap(y + by, NY) * 2 + c, t)

    def per_core(fn):
        for v in (0, 1):
            pl.when(c == v)(functools.partial(fn, v))

    ZK = NZ // 2

    def halved(ref, k, d):
        if k < ZK:
            return ref
        return ref.at[(slice(None),) * (len(ref.shape) - 1) + (pl.ds(d * (D // 2), D // 2),)]

    def ring_start(k, piece, send, recv, base=0, own=None):
        for d, s in enumerate((1, -1)):
            dst = halved(piece(wrap(z - s * (k - 1), NZ)), k, d)
            n = base + 2 * (k - 1) + d
            remote(own if own is not None else dst, dst, send.at[n], recv.at[n], at_z(s)).start()

    def ring_wait(k, piece, send, recv, base=0):
        for d, s in enumerate((1, -1)):
            ref = halved(piece(wrap(z - s * k, NZ)), k, d)
            n = base + 2 * (k - 1) + d
            copy = remote(ref, ref, send.at[n], recv.at[n], at_z(s))
            copy.wait_recv()
            copy.wait_send()

    def arrived(k):
        return [wrap(z - k, NZ)] + ([wrap(z + k, NZ)] if k < ZK else [])

    def group(e):
        return wrap(x - e, NX)

    def w_ring(v, e):
        return lambda o: wg.at[:, group(e), o, v]

    def w_group(v, e):
        return wg.at[:, group(e), :, v]

    def m_ring(v):
        return (lambda o: mg.at[x, o]) if v == 0 else (lambda o: mg.at[:, o])

    def across_start(src, dst, send, recv, peers):
        for e in peers:
            remote(src, dst, send.at[e], recv.at[e], at_x(e)).start()

    def w_across(v, e):
        return w_group(0, e) if v == 0 else wg.at[:, group(e), z, 1]

    def m_across(v, e):
        return mg.at[group(e)] if v == 0 else mg.at[group(e), z]

    def across_wait(ref, recv, e):
        remote(ref, ref, xw_send.at[e], recv.at[e], at_x(e)).wait_recv()

    def to_sibling(v, e):
        return remote(w_group(v, e), w_group(v, e), sw_send.at[e], sw_recv.at[e], sib)

    def from_sibling(e):
        def wait(v):
            to_sibling(1 - v, e).wait_recv()

        per_core(wait)

    lanes = pl.ds(pl.multiple_of(r * 128, 128), 128)

    def first_hop(v):
        own = wq_hbm.at[:, pl.ds(16 * v, 16)]
        ring_start(1, w_ring(v, 0), zw_send, zw_recv, own=own)
        across_start(own, wg.at[:, x, z, v], xw_send, xw_recv, (1, 3) if v == 0 else (1, 3, 2))

    per_core(first_hop)
    own_copies = [
        pltpu.make_async_copy(
            wq_hbm.at[:, pl.ds(pl.multiple_of(16 * c, 16), 16)], wg.at[:, x, z, c], own_sem.at[0]
        ),
        pltpu.make_async_copy(wo_hbm.at[:, lanes], owg.at[x, z, :, lanes], own_sem.at[1]),
        pltpu.make_async_copy(lw_hbm, lwg.at[r], own_sem.at[2]),
    ]
    for copy in own_copies:
        copy.start()

    gain = norm_gain[...]

    @pl.loop(0, F // C)
    def _(i):
        rows = pl.ds(pl.multiple_of(i * C, C), C)
        v = frames[rows, :].astype(F32)
        centred = v - jnp.mean(v, axis=1, keepdims=True)
        spread = jnp.mean(centred * centred, axis=1, keepdims=True)
        normed = (centred * lax.rsqrt(spread + EPS_NORM) * gain).astype(BF)
        xs[rows, :] = normed
        start = first_frame + i * C
        live = start + lax.broadcasted_iota(jnp.int32, (C, 1), 0) < length
        total = jnp.sum(jnp.where(live, normed.astype(F32), 0.0), axis=0, keepdims=True)
        count = jnp.clip(length - start, 1, C).astype(F32)
        mrows[pl.ds(i, 1), :] = total / count

    means = mrows[...]
    power = jnp.mean(means * means, axis=1, keepdims=True)
    mg[x, z] = (means * lax.rsqrt(power + EPS_MEMORY) * memory_gain[...]).astype(BF)

    def memory_hop(v):
        across_start(mg.at[x, z], mg.at[x, z], xm_send, xm_recv, (1, 3, 2))
        if v == 0:
            ring_start(1, m_ring(v), zm_send, zm_recv)
        else:
            for e in (1, 3, 2):
                across_wait(m_across(1, e), xm_recv, e)
            ring_start(1, m_ring(v), zm_send, zm_recv)

    per_core(memory_hop)

    right = remote(
        xs.at[pl.ds(0, 16)], xs.at[pl.ds(F, 16)], r_send.at[0], r_recv.at[0], (r, wrap(t - 1, N_TM))
    )
    right.start()
    for copy in own_copies:
        copy.wait()

    def o_z(o):
        return owg.at[x, o, :, lanes]

    def o_x(e):
        return owg.at[group(e), :, :, lanes]

    def o_y(by, core):
        return owg.at[:, :, :, pl.ds(pl.multiple_of((wrap(y - by, NY) * 2 + core) * 128, 128), 128)]

    for d in range(1, NZ):
        remote(o_z(z), o_z(z), oz_send.at[d], oz_recv.at[d], at_z(d)).start()

    def out_across():
        for d in range(1, NZ):
            ref = o_z(wrap(z - d, NZ))
            remote(ref, ref, oz_send.at[d], oz_recv.at[d], at_z(d)).wait_recv()
        for e in (1, 3, 2):
            remote(o_x(0), o_x(0), ox_send.at[e], ox_recv.at[e], at_x(e)).start()

    def out_up():
        for e in (1, 3, 2):
            remote(o_x(e), o_x(e), ox_send.at[e], ox_recv.at[e], at_x(e)).wait_recv()
        for by in (1, 3, 2):
            remote(o_y(0, c), o_y(0, c), oy_send.at[by], oy_recv.at[by], at_y(by)).start()
        remote(o_y(0, c), o_y(0, c), os_send.at[0], os_recv.at[0], sib).start()

    def out_side():
        for by in (1, 3, 2):
            ref = o_y(by, c)
            remote(ref, ref, oy_send.at[by], oy_recv.at[by], at_y(by)).wait_recv()
            remote(ref, ref, os_send.at[by], os_recv.at[by], sib).start()

    def out_end():
        for by in range(NY):
            ref = o_y(by, 1 - c)
            remote(ref, ref, os_send.at[by], os_recv.at[by], sib).wait_recv()

    lw_up, lw_down, lw_far = (wrap(y + k, NY) * 2 + c for k in (1, -1, 2))

    def lw_half(slot, d):
        return lwg.at[slot, pl.ds(d * (D // 2), D // 2)]

    def hop(ref, k, device=sib):
        return remote(ref, ref, l_send.at[k], l_recv.at[k], device)

    def side(ref, k):
        return remote(ref, ref, ls_send.at[k], ls_recv.at[k], sib)

    hop(lwg.at[r], 0, at_y(1)).start()
    hop(lwg.at[r], 1, at_y(-1)).start()
    side(lwg.at[r], 0).start()

    def lw_step_two():
        hop(lwg.at[lw_down], 0).wait_recv()
        hop(lwg.at[lw_up], 1).wait_recv()
        hop(lw_half(lw_down, 0), 2, at_y(1)).start()
        hop(lw_half(lw_up, 1), 3, at_y(-1)).start()
        side(lwg.at[lw_down], 1).start()
        side(lwg.at[lw_up], 2).start()

    def lw_step_three():
        hop(lw_half(lw_far, 0), 2).wait_recv()
        hop(lw_half(lw_far, 1), 3).wait_recv()
        side(lwg.at[lw_far], 3).start()

    span0 = t * (F // C)

    @pl.loop(0, F // QB)
    def _(b):
        q = b * QB + lax.broadcasted_iota(jnp.int32, (QB, KW), 0)
        n = lax.broadcasted_iota(jnp.int32, (QB, KW), 1)
        q_span = q // C
        u = b * QB + n - MEM
        in_memory = (n < MEM) & (n < span0 + q_span) & (n * C < length)
        same = (u // C) == q_span
        ahead = (u >= (q_span + 1) * C) & (u < (q_span + 1) * C + RC)
        in_frames = (n >= MEM) & (same | ahead) & (first_frame + u < length)
        bias[b] = jnp.where(in_memory | in_frames, 0.0, NEG_BIG)

    own_row = jnp.broadcast_to(owners[...].astype(F32), (TOK, TOK))
    own_col = own_row.T
    earlier = lax.broadcasted_iota(jnp.int32, (TOK, TOK), 0) < lax.broadcasted_iota(
        jnp.int32, (TOK, TOK), 1
    )
    slot = jnp.sum(jnp.where((own_row == own_col) & earlier, 1.0, 0.0), axis=0, keepdims=True)
    target = owners[...].astype(F32) * CAP + slot
    place = lax.broadcasted_iota(jnp.int32, (SLOTS, TOK), 0).astype(F32)
    route = jnp.where(place == target, 1.0, 0.0).astype(BF)
    member = jnp.where(
        lax.broadcasted_iota(jnp.int32, (TOK, F), 0) == segments[...], 1.0, 0.0
    ).astype(BF)
    chosen = dot_nn(route, member)
    ri[...] = chosen.astype(BF)
    cnt[...] = jnp.broadcast_to(
        jnp.maximum(jnp.sum(chosen, axis=1, keepdims=True), 1.0), (SLOTS, 128)
    )
    kk[pl.ds(MEM + F, QB), :] = jnp.zeros((QB, GW), BF)
    vv[pl.ds(MEM + F, QB), :] = jnp.zeros((QB, GW), BF)

    def gather(v):
        for k in range(1, ZK + 1):
            ring_wait(k, w_ring(v, 0), zw_send, zw_recv)
            if k < ZK:
                ring_start(k + 1, w_ring(v, 0), zw_send, zw_recv)
            if v == 0:
                for o in arrived(k):
                    across_start(w_ring(0, 0)(o), w_ring(0, 0)(o), xw_send, xw_recv, (1, 3))
            ring_wait(k, m_ring(v), zm_send, zm_recv)
            if k < ZK:
                ring_start(k + 1, m_ring(v), zm_send, zm_recv)
            if v == 0:
                for o in arrived(k):
                    across_start(mg.at[x, o], mg.at[x, o], xm_send, xm_recv, (1, 3, 2))
            if v == 1 and k == 1:
                for e in (1, 3, 2):
                    across_wait(w_across(1, e), xw_recv, e)
                b_start(1, 1)
                b_start(3, 1)
            if v == 1 and k >= 2:
                b_next(1, k - 1)
                b_next(3, k - 1)
        to_sibling(v, 0).start()
        if v == 0:
            across_start(w_group(0, 0), w_group(0, 0), xw_send, xw_recv, (2,))
            for e in (1, 3, 2):
                across_wait(m_across(0, e), xm_recv, e)

    def b_start(e, k):
        ring_start(k, w_ring(1, e), zw_send, zw_recv, base=8 * e)

    def b_next(e, k):
        ring_wait(k, w_ring(1, e), zw_send, zw_recv, base=8 * e)
        if k < ZK:
            b_start(e, k + 1)
        else:
            to_sibling(1, e).start()

    def x_next(e):
        across_wait(w_across(0, e), xw_recv, e)
        to_sibling(0, e).start()

    per_core(gather)
    out_across()
    lw_step_two()
    right.wait()

    def hook_0q(v):
        if v == 1:
            b_next(1, 4)
            b_next(3, 4)
            b_start(2, 1)
        else:
            x_next(1)

    def hook_0a(v):
        if v == 1:
            b_next(2, 1)
        else:
            x_next(3)

    def hook_1q(v):
        if v == 1:
            b_next(2, 2)

    def hook_1a(v):
        if v == 1:
            b_next(2, 3)

    def hook_2q(v):
        if v == 1:
            b_next(2, 4)
        else:
            x_next(2)

    def after_projection(j):
        @pl.when(j == 0)
        def _():
            per_core(hook_0q)

        @pl.when(j == 1)
        def _():
            per_core(hook_1q)

        @pl.when(j == 2)
        def _():
            per_core(hook_2q)

        @pl.when(j == 3)
        def _():
            out_side()

    def after_attention(j):
        @pl.when(j == 0)
        def _():
            per_core(hook_0a)
            out_up()

        @pl.when(j == 1)
        def _():
            per_core(hook_1a)
            lw_step_three()

    lane_head = lax.broadcasted_iota(jnp.int32, (1, GW), 1) // HEAD

    @pl.loop(0, G)
    def _(j):
        for jj, e in enumerate((0, 1, 3, 2)):
            pl.when(j == jj)(functools.partial(from_sibling, e))
        g = wrap(x - (j + (j // 2) * (5 - 2 * j)), NX)
        a = xs[...]
        q = dot_nt(a, wg[0, g].reshape(GW, D))[:F] * (HEAD**-0.5 * LOG2E)
        for h in range(4):
            q4[:, h * QB : (h + 1) * QB, :] = (
                jnp.where(lane_head == h, q, 0.0).astype(BF).reshape(F // QB, QB, GW)
            )
        m = mg[...].reshape(MEM, D)
        for n, ref in ((1, kk), (2, vv)):
            w = wg[n, g].reshape(GW, D)
            ref[pl.ds(MEM, F + 16), :] = dot_nt(a, w).astype(BF)
            ref[pl.ds(0, MEM), :] = dot_nt(m, w).astype(BF)
        after_projection(j)
        columns = pl.ds(pl.multiple_of(g * GW, GW), GW)
        for b in range(F // QB):
            near = pl.ds(MEM + b * QB, 2 * QB)
            q = q4[b]
            s = jnp.concatenate([dot_nt(q, kk[pl.ds(0, MEM), :]), dot_nt(q, kk[near, :])], axis=1)
            s = (s.reshape(4, QB, KW) + bias[b][None]).reshape(4 * QB, KW)
            peak = jnp.max(s, axis=1, keepdims=True)
            w = jnp.exp2(s - peak)
            total = jnp.sum(w, axis=1, keepdims=True)
            w = w.astype(BF)
            o = dot_nn(w[:, :MEM], vv[pl.ds(0, MEM), :]) + dot_nn(w[:, MEM:], vv[near, :])
            o, total = o.reshape(4, QB, GW), total.reshape(4, QB, 1)
            out, den = o[3], jnp.broadcast_to(total[3], (QB, GW))
            for h in range(3):
                out = jnp.where(lane_head == h, o[h], out)
                den = jnp.where(lane_head == h, total[h], den)
            att[b * QB : (b + 1) * QB, columns] = (out / den).astype(BF)
        after_attention(j)

    out_end()

    for ch in range(NCH):
        features = slice(ch * CH, (ch + 1) * CH)
        w = owg[pl.ds(ch * (NX // NCH), NX // NCH)].reshape(CH, D)
        for b in range(2):
            rows = slice(b * 256, (b + 1) * 256)
            o = dot_nt(att[rows, :], w)
            live = first_frame + b * 256 + lax.broadcasted_iota(jnp.int32, (256, 1), 0) < length
            enc[rows, features] = jnp.where(
                live, frames[rows, features].astype(F32) + o, 0.0
            ).astype(BF)
        sent = dot_nn(ri[...], enc[:, features]) / cnt[:, :1]
        sb[ch] = sent.reshape(N_TM, CAP, CH).astype(BF)

        @pl.loop(1, N_TM)
        def _(d):
            to = lax.rem(t + d, N_TM)
            remote(sb.at[ch, to], rb.at[ch, t], a_send.at[ch, d], a_recv.at[ch, d], (r, to)).start()

        rb[ch, t] = sb[ch, t]

    enc_out = pltpu.make_async_copy(enc, enc_hbm, out_sem.at[0])
    enc_out.start()

    def sent_core(v):
        for e in (1, 2, 3):
            ref = w_group(0, 0) if v == 0 else wg.at[:, x, z, 1]
            remote(ref, ref, xw_send.at[e], xw_recv.at[e], sib).wait_send()
            ref = mg.at[x] if v == 0 else mg.at[x, z]
            remote(ref, ref, xm_send.at[e], xm_recv.at[e], sib).wait_send()
        for e in range(NX):
            to_sibling(v, e).wait_send()

    per_core(sent_core)
    for d in range(1, NZ):
        remote(o_z(z), o_z(z), oz_send.at[d], oz_recv.at[d], sib).wait_send()
    for e in (1, 2, 3):
        remote(o_x(0), o_x(0), ox_send.at[e], ox_recv.at[e], sib).wait_send()
        remote(o_y(0, c), o_y(0, c), oy_send.at[e], oy_recv.at[e], sib).wait_send()
    for by in range(NY):
        ref = o_y(by, c)
        remote(ref, ref, os_send.at[by], os_recv.at[by], sib).wait_send()
    for k, slot in enumerate((r, lw_down, lw_up, lw_far)):
        side(lwg.at[slot], k).wait_send()
        side(lwg.at[slot + 1 - 2 * c], k).wait_recv()
    hop(lwg.at[r], 0).wait_send()
    hop(lwg.at[r], 1).wait_send()
    hop(lw_half(r, 0), 2).wait_send()
    hop(lw_half(r, 0), 3).wait_send()

    for ch in range(NCH):

        @pl.loop(1, N_TM)
        def _(d):
            to = lax.rem(t + d, N_TM)
            source = wrap(t - d, N_TM)
            copy = remote(
                sb.at[ch, to], rb.at[ch, source], a_send.at[ch, d], a_recv.at[ch, d], (r, to)
            )
            copy.wait_recv()
            copy.wait_send()

        got = rb[ch].astype(F32).reshape(SLOTS, CH).astype(BF)
        for k in range(2 * NY):
            part = dot_nn(got, lwg[k, ch * CH : (ch + 1) * CH, :])
            if ch > 0:
                part += lacc[k]
            if ch < NCH - 1:
                lacc[k] = part
            else:
                lmo[:, k * 256 : (k + 1) * 256] = part.astype(BF)
    lm_out = pltpu.make_async_copy(lmo, lm_hbm, out_sem.at[1])
    lm_out.start()
    enc_out.wait()
    lm_out.wait()


def per_device(
    frames, lengths, norm_gain, memory_gain, qkv_weight, out_weight, segment_ids, owners, language_weight
):
    vmem = pl.BlockSpec(memory_space=pltpu.VMEM)
    smem = pl.BlockSpec(memory_space=pltpu.SMEM)
    hbm = pl.BlockSpec(memory_space=pl.ANY)
    dma = pltpu.SemaphoreType.DMA
    enc, lm = pl.pallas_call(
        kernel,
        out_shape=(
            jax.ShapeDtypeStruct((F, D), BF),
            jax.ShapeDtypeStruct((SLOTS, DL), BF),
        ),
        in_specs=[vmem, smem, vmem, vmem, hbm, hbm, vmem, vmem, hbm],
        out_specs=(hbm, hbm),
        scratch_shapes=[
            pltpu.VMEM((3, NX, NZ, 2, 16, D), BF),
            pltpu.VMEM((NX, NZ, 32, D), BF),
            pltpu.VMEM((2 * NY, D, DL // (2 * NY)), BF),
            pltpu.VMEM((F + 16, D), BF),
            pltpu.VMEM((NX, NZ, 16, D), BF),
            pltpu.VMEM((F // C, D), F32),
            pltpu.VMEM((F // QB, 4 * QB, GW), BF),
            pltpu.VMEM((MEM + F + QB, GW), BF),
            pltpu.VMEM((MEM + F + QB, GW), BF),
            pltpu.VMEM((F, D), BF),
            pltpu.VMEM((F // QB, QB, KW), F32),
            pltpu.VMEM((SLOTS, F), BF),
            pltpu.VMEM((SLOTS, 128), F32),
            pltpu.VMEM((F, D), BF),
            pltpu.VMEM((NCH, N_TM, CAP, CH), BF),
            pltpu.VMEM((NCH, N_TM, CAP, CH), BF),
            pltpu.VMEM((2 * NY, SLOTS, 256), F32),
            pltpu.VMEM((SLOTS, DL), BF),
            dma((32,)), dma((32,)), dma((8,)), dma((8,)), dma((4,)), dma((4,)), dma((4,)), dma((4,)),
            dma((4,)), dma((4,)),
            dma((8,)), dma((8,)), dma((4,)), dma((4,)), dma((4,)), dma((4,)), dma((4,)), dma((4,)),
            dma((1,)), dma((1,)), dma((4,)), dma((4,)), dma((4,)), dma((4,)),
            dma((NCH, N_TM)), dma((NCH, N_TM)), dma((3,)), dma((2,)),
        ],
        compiler_params=pltpu.CompilerParams(
            collective_id=0, has_side_effects=True, vmem_limit_bytes=58 * 2**20
        ),
        name="block",
    )(
        frames[0],
        lengths,
        norm_gain[None],
        memory_gain[None],
        qkv_weight.transpose(0, 2, 1),
        out_weight.T,
        segment_ids[0],
        owners[0, :, :, 0],
        language_weight,
    )
    return (enc[None], lm[None, None])


def solution(mesh):
    in_specs = (
        P("rec", "tm", None),
        P("rec"),
        P(),
        P(),
        P(None, None, "tm"),
        P(None, "tm"),
        P("rec", "tm", None),
        P("rec", "tm", None, None),
        P(None, "rec"),
    )
    out_specs = (P("rec", "tm", None), P("rec", "tm", None, None))
    return jax.shard_map(
        per_device, mesh=mesh, in_specs=in_specs, out_specs=out_specs, check_vma=False
    )
```

time: 110 us -> 89.6 us (0.81)
  the two profiles are of different devices: /device:TPU:1 before, /device:TPU:18 now
where the time goes in v2:
time: 89.6 us; the launch traced here: 89.5 us
  Pallas kernels  84.8 us (95%)
  local copies, waits for them, and re-layouts  3.32 us (4%)
  between operations  1.29 us (1%)
    pallas_call x1, Pallas kernels, per_device(): pl.pallas_call(kernel, out_shape=(jax.ShapeDtypeStruct((F, D), BF), jax.S...  84.8 us
    unnamed x4, local copies, waits for them, and re-layouts  3.32 us

profile of v2, /device:TPU:18, one launch (start us, length us, event | category | flops | bytes accessed | tf_op | source)
XLA Modules:
  0.0 89.5 jit_solution(16176524848243105964)
XLA Ops:
  1.3 84.8 %block.1 = (bf16[512,1024]{1,0:T(8,128)(2,1)}, bf16[256,2048]{1,0:T(8,128)(2,1)}) custom-call(bf16[512,1024]{1,0:T(8,128)(2,1)} %bitcast.9, s32[1]{0:T(128)S(6)} %copy.13.lengths, f32[1,1024]{1,0:T(1,128)} %bitcast.14, f32[1,1024]{1,0:T(1,128)} %bitcast.15, bf16[3,32,1024]{2,1,0:T(8,128)(2,1)} %bitcast.12, bf16[32,1024]{1,0:T(8,128)(2,1)} %bitcast.13, ...), custom_call_target="tpu_custom_call" | custom-call | tf_op jit(solution)/shard_map/block/pallas_call | solution.py:544
  86.1 0.0 copy-start
  86.1 2.4 %copy.14 = bf16[1,512,1024]{2,1,0:T(8,128)(2,1)} copy(bf16[1,512,1024]{2,1,0:T(8,128)(2,1)} %bitcast.11) | data formatting | bytes 2097152
  88.5 0.0 copy-done
  88.5 1.0 %copy.15 = bf16[1,1,256,2048]{3,2,1,0:T(8,128)(2,1)} copy(bf16[1,1,256,2048]{3,2,1,0:T(8,128)(2,1)S(1)} %bitcast.10) | data formatting | bytes 2097152
Async XLA Ops:
  86.1 2.4 %copy-start = (bf16[256,2048]{1,0:T(8,128)(2,1)S(1)}, bf16[256,2048]{1,0:T(8,128)(2,1)}, u32[]{:S(2)}) copy-start(bf16[256,2048]{1,0:T(8,128)(2,1)} %get-tuple-element.5) | copy-start | bytes 3145732

commit v3 on v2

--- a/solution.py
+++ b/solution.py
@@ -52,6 +52,7 @@
     enc_hbm, lm_hbm,
     wg, owg, lwg, xs, mg, mrows, q4, kk, vv, att, bias, ri, cnt, enc, sb, rb, lacc, lmo,
     zw_send, zw_recv, zm_send, zm_recv, xw_send, xw_recv, xm_send, xm_recv, sw_send, sw_recv,
+    x2_send, x2_recv, z2_send, z2_recv, y2_send, y2_recv, s2_send, s2_recv,
     oz_send, oz_recv, ox_send, ox_recv, oy_send, oy_recv, os_send, os_recv,
     r_send, r_recv, l_send, l_recv, ls_send, ls_recv, a_send, a_recv, own_sem, out_sem,
 ):
@@ -109,16 +110,16 @@
             return ref
         return ref.at[(slice(None),) * (len(ref.shape) - 1) + (pl.ds(d * (D // 2), D // 2),)]
 
-    def ring_start(k, piece, send, recv, base=0, own=None):
+    def ring_start(k, piece, send, recv, own=None):
         for d, s in enumerate((1, -1)):
             dst = halved(piece(wrap(z - s * (k - 1), NZ)), k, d)
-            n = base + 2 * (k - 1) + d
+            n = 2 * (k - 1) + d
             remote(own if own is not None else dst, dst, send.at[n], recv.at[n], at_z(s)).start()
 
-    def ring_wait(k, piece, send, recv, base=0):
+    def ring_wait(k, piece, send, recv):
         for d, s in enumerate((1, -1)):
             ref = halved(piece(wrap(z - s * k, NZ)), k, d)
-            n = base + 2 * (k - 1) + d
+            n = 2 * (k - 1) + d
             copy = remote(ref, ref, send.at[n], recv.at[n], at_z(s))
             copy.wait_recv()
             copy.wait_send()
@@ -143,7 +144,7 @@
             remote(src, dst, send.at[e], recv.at[e], at_x(e)).start()
 
     def w_across(v, e):
-        return w_group(0, e) if v == 0 else wg.at[:, group(e), z, 1]
+        return w_group(v, e)
 
     def m_across(v, e):
         return mg.at[group(e)] if v == 0 else mg.at[group(e), z]
@@ -163,14 +164,18 @@
     lanes = pl.ds(pl.multiple_of(r * 128, 128), 128)
 
     def first_hop(v):
-        own = wq_hbm.at[:, pl.ds(16 * v, 16)]
+        own = wq_hbm.at[:, v]
         ring_start(1, w_ring(v, 0), zw_send, zw_recv, own=own)
-        across_start(own, wg.at[:, x, z, v], xw_send, xw_recv, (1, 3) if v == 0 else (1, 3, 2))
+        across_start(own, wg.at[:, x, z, v], xw_send, xw_recv, (1, 3))
 
     per_core(first_hop)
+    far_first = remote(
+        wq_hbm.at[:, :, :, lanes], wg.at[:, x, z, :, :, lanes], x2_send.at[0], x2_recv.at[0], at_x(2)
+    )
+    far_first.start()
     own_copies = [
         pltpu.make_async_copy(
-            wq_hbm.at[:, pl.ds(pl.multiple_of(16 * c, 16), 16)], wg.at[:, x, z, c], own_sem.at[0]
+            wq_hbm.at[:, c], wg.at[:, x, z, c], own_sem.at[0]
         ),
         pltpu.make_async_copy(wo_hbm.at[:, lanes], owg.at[x, z, :, lanes], own_sem.at[1]),
         pltpu.make_async_copy(lw_hbm, lwg.at[r], own_sem.at[2]),
@@ -198,23 +203,37 @@
     power = jnp.mean(means * means, axis=1, keepdims=True)
     mg[x, z] = (means * lax.rsqrt(power + EPS_MEMORY) * memory_gain[...]).astype(BF)
 
-    def memory_hop(v):
+    def round_one(v):
+        ring_next(v, 1)
         across_start(mg.at[x, z], mg.at[x, z], xm_send, xm_recv, (1, 3, 2))
         if v == 0:
             ring_start(1, m_ring(v), zm_send, zm_recv)
+
+    def ring_next(v, k):
+        ring_wait(k, w_ring(v, 0), zw_send, zw_recv)
+        if k < ZK:
+            ring_start(k + 1, w_ring(v, 0), zw_send, zw_recv)
         else:
-            for e in (1, 3, 2):
-                across_wait(m_across(1, e), xm_recv, e)
-            ring_start(1, m_ring(v), zm_send, zm_recv)
-
-    per_core(memory_hop)
+            to_sibling(v, 0).start()
+        for o in arrived(k):
+            across_start(w_ring(v, 0)(o), w_ring(v, 0)(o), xw_send, xw_recv, (1, 3))
+
+    def memory_next(v, k):
+        ring_wait(k, m_ring(v), zm_send, zm_recv)
+        if k < ZK:
+            ring_start(k + 1, m_ring(v), zm_send, zm_recv)
+        if v == 0:
+            for o in arrived(k):
+                across_start(mg.at[x, o], mg.at[x, o], xm_send, xm_recv, (1, 3, 2))
+
+    for copy in own_copies:
+        copy.wait()
+    per_core(round_one)
 
     right = remote(
         xs.at[pl.ds(0, 16)], xs.at[pl.ds(F, 16)], r_send.at[0], r_recv.at[0], (r, wrap(t - 1, N_TM))
     )
     right.start()
-    for copy in own_copies:
-        copy.wait()
 
     def o_z(o):
         return owg.at[x, o, :, lanes]
@@ -315,127 +334,151 @@
     kk[pl.ds(MEM + F, QB), :] = jnp.zeros((QB, GW), BF)
     vv[pl.ds(MEM + F, QB), :] = jnp.zeros((QB, GW), BF)
 
-    def gather(v):
-        for k in range(1, ZK + 1):
-            ring_wait(k, w_ring(v, 0), zw_send, zw_recv)
-            if k < ZK:
-                ring_start(k + 1, w_ring(v, 0), zw_send, zw_recv)
-            if v == 0:
-                for o in arrived(k):
-                    across_start(w_ring(0, 0)(o), w_ring(0, 0)(o), xw_send, xw_recv, (1, 3))
-            ring_wait(k, m_ring(v), zm_send, zm_recv)
-            if k < ZK:
-                ring_start(k + 1, m_ring(v), zm_send, zm_recv)
-            if v == 0:
-                for o in arrived(k):
-                    across_start(mg.at[x, o], mg.at[x, o], xm_send, xm_recv, (1, 3, 2))
-            if v == 1 and k == 1:
-                for e in (1, 3, 2):
-                    across_wait(w_across(1, e), xw_recv, e)
-                b_start(1, 1)
-                b_start(3, 1)
-            if v == 1 and k >= 2:
-                b_next(1, k - 1)
-                b_next(3, k - 1)
-        to_sibling(v, 0).start()
-        if v == 0:
-            across_start(w_group(0, 0), w_group(0, 0), xw_send, xw_recv, (2,))
+    def round_two(v):
+        if v == 1:
+            for e in (1, 3, 2):
+                across_wait(m_across(1, e), xm_recv, e)
+            ring_start(1, m_ring(v), zm_send, zm_recv)
+        else:
+            memory_next(v, 1)
+        ring_next(v, 2)
+
+    def round_three(v):
+        if v == 1:
+            memory_next(v, 1)
+            ring_next(v, 3)
+        else:
+            ring_next(v, 3)
+            memory_next(v, 2)
+
+    def round_four(v):
+        if v == 1:
+            memory_next(v, 2)
+            ring_next(v, 4)
+        else:
+            ring_next(v, 4)
+            memory_next(v, 3)
+
+    def round_five(v):
+        memory_next(v, 3 if v == 1 else 4)
+
+    def round_six(v):
+        if v == 1:
+            memory_next(v, 4)
+        else:
             for e in (1, 3, 2):
                 across_wait(m_across(0, e), xm_recv, e)
 
-    def b_start(e, k):
-        ring_start(k, w_ring(1, e), zw_send, zw_recv, base=8 * e)
-
-    def b_next(e, k):
-        ring_wait(k, w_ring(1, e), zw_send, zw_recv, base=8 * e)
-        if k < ZK:
-            b_start(e, k + 1)
-        else:
-            to_sibling(1, e).start()
-
     def x_next(e):
-        across_wait(w_across(0, e), xw_recv, e)
-        to_sibling(0, e).start()
-
-    per_core(gather)
+        def one(v):
+            across_wait(w_across(v, e), xw_recv, e)
+            to_sibling(v, e).start()
+
+        per_core(one)
+
+    def far_piece(rec):
+        return wg.at[:, group(2), :, :, :, pl.ds(pl.multiple_of(rec * 128, 128), 128)]
+
+    def far_z(o):
+        return wg.at[:, group(2), o, :, :, lanes]
+
+    def far_along():
+        remote(far_z(z), far_z(z), x2_send.at[0], x2_recv.at[0], at_x(2)).wait_recv()
+        for d in (4, 3, 5, 2, 6, 1, 7):
+            remote(far_z(z), far_z(z), z2_send.at[d], z2_recv.at[d], at_z(d)).start()
+
+    def far_up():
+        for d in range(1, NZ):
+            ref = far_z(wrap(z - d, NZ))
+            remote(ref, ref, z2_send.at[d], z2_recv.at[d], at_z(d)).wait_recv()
+        ref = far_piece(r)
+        for by in (1, 3, 2):
+            remote(ref, ref, y2_send.at[by], y2_recv.at[by], at_y(by)).start()
+        remote(ref, ref, s2_send.at[0], s2_recv.at[0], sib).start()
+
+    def far_side():
+        for by in (1, 3, 2):
+            ref = far_piece(wrap(y - by, NY) * 2 + c)
+            remote(ref, ref, y2_send.at[by], y2_recv.at[by], at_y(by)).wait_recv()
+            remote(ref, ref, s2_send.at[by], s2_recv.at[by], sib).start()
+
+    def far_end():
+        for by in range(NY):
+            ref = far_piece(wrap(y - by, NY) * 2 + 1 - c)
+            remote(ref, ref, s2_send.at[by], s2_recv.at[by], sib).wait_recv()
+
+    per_core(round_two)
     out_across()
-    lw_step_two()
+    per_core(round_three)
+    per_core(round_four)
+    out_up()
+    far_along()
+    per_core(round_five)
+    from_sibling(0)
     right.wait()
-
-    def hook_0q(v):
-        if v == 1:
-            b_next(1, 4)
-            b_next(3, 4)
-            b_start(2, 1)
-        else:
-            x_next(1)
-
-    def hook_0a(v):
-        if v == 1:
-            b_next(2, 1)
-        else:
-            x_next(3)
-
-    def hook_1q(v):
-        if v == 1:
-            b_next(2, 2)
-
-    def hook_1a(v):
-        if v == 1:
-            b_next(2, 3)
-
-    def hook_2q(v):
-        if v == 1:
-            b_next(2, 4)
-        else:
-            x_next(2)
-
-    def after_projection(j):
-        @pl.when(j == 0)
-        def _():
-            per_core(hook_0q)
-
-        @pl.when(j == 1)
-        def _():
-            per_core(hook_1q)
-
-        @pl.when(j == 2)
-        def _():
-            per_core(hook_2q)
-
-        @pl.when(j == 3)
-        def _():
-            out_side()
-
-    def after_attention(j):
-        @pl.when(j == 0)
-        def _():
-            per_core(hook_0a)
-            out_up()
-
-        @pl.when(j == 1)
-        def _():
-            per_core(hook_1a)
-            lw_step_three()
-
     lane_head = lax.broadcasted_iota(jnp.int32, (1, GW), 1) // HEAD
 
-    @pl.loop(0, G)
-    def _(j):
-        for jj, e in enumerate((0, 1, 3, 2)):
-            pl.when(j == jj)(functools.partial(from_sibling, e))
-        g = wrap(x - (j + (j // 2) * (5 - 2 * j)), NX)
+    def project_frames(g):
         a = xs[...]
         q = dot_nt(a, wg[0, g].reshape(GW, D))[:F] * (HEAD**-0.5 * LOG2E)
         for h in range(4):
             q4[:, h * QB : (h + 1) * QB, :] = (
                 jnp.where(lane_head == h, q, 0.0).astype(BF).reshape(F // QB, QB, GW)
             )
+        for n, ref in ((1, kk), (2, vv)):
+            ref[pl.ds(MEM, F + 16), :] = dot_nt(a, wg[n, g].reshape(GW, D)).astype(BF)
+
+    project_frames(x)
+    per_core(round_six)
+
+    def before_projection(j):
+        @pl.when(j == 1)
+        def _():
+            from_sibling(1)
+
+        @pl.when(j == 2)
+        def _():
+            from_sibling(3)
+
+        @pl.when(j == 3)
+        def _():
+            far_end()
+
+    def after_projection(j):
+        @pl.when(j == 0)
+        def _():
+            x_next(1)
+            far_up()
+
+        @pl.when(j == 1)
+        def _():
+            out_side()
+
+        @pl.when(j == 3)
+        def _():
+            lw_step_two()
+
+    def after_attention(j):
+        @pl.when(j == 0)
+        def _():
+            x_next(3)
+
+        @pl.when(j == 2)
+        def _():
+            far_side()
+
+    @pl.loop(0, G)
+    def _(j):
+        before_projection(j)
+        g = wrap(x - (j + (j // 2) * (5 - 2 * j)), NX)
+
+        @pl.when(j > 0)
+        def _():
+            project_frames(g)
+
         m = mg[...].reshape(MEM, D)
         for n, ref in ((1, kk), (2, vv)):
-            w = wg[n, g].reshape(GW, D)
-            ref[pl.ds(MEM, F + 16), :] = dot_nt(a, w).astype(BF)
-            ref[pl.ds(0, MEM), :] = dot_nt(m, w).astype(BF)
+            ref[pl.ds(0, MEM), :] = dot_nt(m, wg[n, g].reshape(GW, D)).astype(BF)
         after_projection(j)
         columns = pl.ds(pl.multiple_of(g * GW, GW), GW)
         for b in range(F // QB):
@@ -480,17 +523,27 @@
 
     enc_out = pltpu.make_async_copy(enc, enc_hbm, out_sem.at[0])
     enc_out.start()
+    lw_step_three()
 
     def sent_core(v):
         for e in (1, 2, 3):
-            ref = w_group(0, 0) if v == 0 else wg.at[:, x, z, 1]
-            remote(ref, ref, xw_send.at[e], xw_recv.at[e], sib).wait_send()
+            if e != 2:
+                ref = w_group(v, 0)
+                remote(ref, ref, xw_send.at[e], xw_recv.at[e], sib).wait_send()
             ref = mg.at[x] if v == 0 else mg.at[x, z]
             remote(ref, ref, xm_send.at[e], xm_recv.at[e], sib).wait_send()
-        for e in range(NX):
+        for e in (0, 1, 3):
             to_sibling(v, e).wait_send()
 
     per_core(sent_core)
+    remote(far_z(z), far_z(z), x2_send.at[0], x2_recv.at[0], sib).wait_send()
+    for d in range(1, NZ):
+        remote(far_z(z), far_z(z), z2_send.at[d], z2_recv.at[d], sib).wait_send()
+    for by in range(NY):
+        ref = far_piece(wrap(y - by, NY) * 2 + c)
+        remote(ref, ref, s2_send.at[by], s2_recv.at[by], sib).wait_send()
+        if by:
+            remote(ref, ref, y2_send.at[by], y2_recv.at[by], sib).wait_send()
     for d in range(1, NZ):
         remote(o_z(z), o_z(z), oz_send.at[d], oz_recv.at[d], sib).wait_send()
     for e in (1, 2, 3):
@@ -507,6 +560,11 @@
     hop(lw_half(r, 0), 2).wait_send()
     hop(lw_half(r, 0), 3).wait_send()
 
+    def lm_out(k):
+        return pltpu.make_async_copy(
+            lmo.at[k], lm_hbm.at[:, pl.ds(k * 256, 256)], out_sem.at[1 + k]
+        )
+
     for ch in range(NCH):
 
         @pl.loop(1, N_TM)
@@ -527,11 +585,11 @@
             if ch < NCH - 1:
                 lacc[k] = part
             else:
-                lmo[:, k * 256 : (k + 1) * 256] = part.astype(BF)
-    lm_out = pltpu.make_async_copy(lmo, lm_hbm, out_sem.at[1])
-    lm_out.start()
+                lmo[k] = part.astype(BF)
+                lm_out(k).start()
     enc_out.wait()
-    lm_out.wait()
+    for k in range(2 * NY):
+        lm_out(k).wait()
 
 
 def per_device(
@@ -567,12 +625,13 @@
             pltpu.VMEM((NCH, N_TM, CAP, CH), BF),
             pltpu.VMEM((NCH, N_TM, CAP, CH), BF),
             pltpu.VMEM((2 * NY, SLOTS, 256), F32),
-            pltpu.VMEM((SLOTS, DL), BF),
-            dma((32,)), dma((32,)), dma((8,)), dma((8,)), dma((4,)), dma((4,)), dma((4,)), dma((4,)),
+            pltpu.VMEM((2 * NY, SLOTS, DL // (2 * NY)), BF),
+            dma((8,)), dma((8,)), dma((8,)), dma((8,)), dma((4,)), dma((4,)), dma((4,)), dma((4,)),
             dma((4,)), dma((4,)),
+            dma((1,)), dma((1,)), dma((8,)), dma((8,)), dma((4,)), dma((4,)), dma((4,)), dma((4,)),
             dma((8,)), dma((8,)), dma((4,)), dma((4,)), dma((4,)), dma((4,)), dma((4,)), dma((4,)),
             dma((1,)), dma((1,)), dma((4,)), dma((4,)), dma((4,)), dma((4,)),
-            dma((NCH, N_TM)), dma((NCH, N_TM)), dma((3,)), dma((2,)),
+            dma((NCH, N_TM)), dma((NCH, N_TM)), dma((3,)), dma((1 + 2 * NY,)),
         ],
         compiler_params=pltpu.CompilerParams(
             collective_id=0, has_side_effects=True, vmem_limit_bytes=58 * 2**20
@@ -583,7 +642,7 @@
         lengths,
         norm_gain[None],
         memory_gain[None],
-        qkv_weight.transpose(0, 2, 1),
+        qkv_weight.transpose(0, 2, 1).reshape(3, 2, 16, D),
         out_weight.T,
         segment_ids[0],
         owners[0, :, :, 0],

time: 89.6 us -> 84.5 us (0.943)
  the two profiles are of different devices: /device:TPU:18 before, /device:TPU:1 now
where the time goes in v3:
time: 84.5 us; the launch traced here: 84.3 us
  Pallas kernels  79.7 us (94%)
  local copies, waits for them, and re-layouts  3.32 us (4%)
  between operations  1.29 us (2%)
    pallas_call x1, Pallas kernels, per_device(): pl.pallas_call(kernel, out_shape=(jax.ShapeDtypeStruct((F, D), BF), jax.S...  79.7 us
    unnamed x4, local copies, waits for them, and re-layouts  3.32 us

profile of v3, /device:TPU:1, one launch (start us, length us, event | category | flops | bytes accessed | tf_op | source)
XLA Modules:
  0.0 84.3 jit_solution(8302846395599119610)
XLA Ops:
  1.3 79.7 %block.1 = (bf16[512,1024]{1,0:T(8,128)(2,1)}, bf16[256,2048]{1,0:T(8,128)(2,1)}) custom-call(bf16[512,1024]{1,0:T(8,128)(2,1)} %bitcast.11, s32[1]{0:T(128)S(6)} %copy.13.lengths, f32[1,1024]{1,0:T(1,128)} %bitcast.16, f32[1,1024]{1,0:T(1,128)} %bitcast.17, bf16[3,2,16,1024]{3,2,1,0:T(8,128)(2,1)} %bitcast.14, bf16[32,1024]{1,0:T(8,128)(2,1)} %bitcast.15, ...), custom_call_target="tpu_custom_call" | custom-call | tf_op jit(solution)/shard_map/block/pallas_call | solution.py:602
  81.0 0.0 copy-start
  81.0 2.4 %copy.14 = bf16[1,512,1024]{2,1,0:T(8,128)(2,1)} copy(bf16[1,512,1024]{2,1,0:T(8,128)(2,1)} %bitcast.13) | data formatting | bytes 2097152
  83.3 0.0 copy-done
  83.3 1.0 %copy.15 = bf16[1,1,256,2048]{3,2,1,0:T(8,128)(2,1)} copy(bf16[1,1,256,2048]{3,2,1,0:T(8,128)(2,1)S(1)} %bitcast.12) | data formatting | bytes 2097152
Async XLA Ops:
  81.0 2.4 %copy-start = (bf16[256,2048]{1,0:T(8,128)(2,1)S(1)}, bf16[256,2048]{1,0:T(8,128)(2,1)}, u32[]{:S(2)}) copy-start(bf16[256,2048]{1,0:T(8,128)(2,1)} %get-tuple-element.5) | copy-start | bytes 3145732

commit v4 on v3

--- a/solution.py
+++ b/solution.py
@@ -78,228 +78,6 @@
             barrier, inc=1, device_id=(lax.rem(r + d, 2 * NY), t), device_id_type=pl.DeviceIdType.MESH
         )
 
-    pl.semaphore_wait(barrier, N_TM - 1 + 2 * NY - 1)
-
-    def remote(src, dst, send, recv, device):
-        return pltpu.make_async_remote_copy(
-            src_ref=src,
-            dst_ref=dst,
-            send_sem=send,
-            recv_sem=recv,
-            device_id=device,
-            device_id_type=pl.DeviceIdType.MESH,
-        )
-
-    def at_z(by):
-        return (r, x * NZ + wrap(z + by, NZ))
-
-    def at_x(by):
-        return (r, wrap(x + by, NX) * NZ + z)
-
-    def at_y(by):
-        return (wrap(y + by, NY) * 2 + c, t)
-
-    def per_core(fn):
-        for v in (0, 1):
-            pl.when(c == v)(functools.partial(fn, v))
-
-    ZK = NZ // 2
-
-    def halved(ref, k, d):
-        if k < ZK:
-            return ref
-        return ref.at[(slice(None),) * (len(ref.shape) - 1) + (pl.ds(d * (D // 2), D // 2),)]
-
-    def ring_start(k, piece, send, recv, own=None):
-        for d, s in enumerate((1, -1)):
-            dst = halved(piece(wrap(z - s * (k - 1), NZ)), k, d)
-            n = 2 * (k - 1) + d
-            remote(own if own is not None else dst, dst, send.at[n], recv.at[n], at_z(s)).start()
-
-    def ring_wait(k, piece, send, recv):
-        for d, s in enumerate((1, -1)):
-            ref = halved(piece(wrap(z - s * k, NZ)), k, d)
-            n = 2 * (k - 1) + d
-            copy = remote(ref, ref, send.at[n], recv.at[n], at_z(s))
-            copy.wait_recv()
-            copy.wait_send()
-
-    def arrived(k):
-        return [wrap(z - k, NZ)] + ([wrap(z + k, NZ)] if k < ZK else [])
-
-    def group(e):
-        return wrap(x - e, NX)
-
-    def w_ring(v, e):
-        return lambda o: wg.at[:, group(e), o, v]
-
-    def w_group(v, e):
-        return wg.at[:, group(e), :, v]
-
-    def m_ring(v):
-        return (lambda o: mg.at[x, o]) if v == 0 else (lambda o: mg.at[:, o])
-
-    def across_start(src, dst, send, recv, peers):
-        for e in peers:
-            remote(src, dst, send.at[e], recv.at[e], at_x(e)).start()
-
-    def w_across(v, e):
-        return w_group(v, e)
-
-    def m_across(v, e):
-        return mg.at[group(e)] if v == 0 else mg.at[group(e), z]
-
-    def across_wait(ref, recv, e):
-        remote(ref, ref, xw_send.at[e], recv.at[e], at_x(e)).wait_recv()
-
-    def to_sibling(v, e):
-        return remote(w_group(v, e), w_group(v, e), sw_send.at[e], sw_recv.at[e], sib)
-
-    def from_sibling(e):
-        def wait(v):
-            to_sibling(1 - v, e).wait_recv()
-
-        per_core(wait)
-
-    lanes = pl.ds(pl.multiple_of(r * 128, 128), 128)
-
-    def first_hop(v):
-        own = wq_hbm.at[:, v]
-        ring_start(1, w_ring(v, 0), zw_send, zw_recv, own=own)
-        across_start(own, wg.at[:, x, z, v], xw_send, xw_recv, (1, 3))
-
-    per_core(first_hop)
-    far_first = remote(
-        wq_hbm.at[:, :, :, lanes], wg.at[:, x, z, :, :, lanes], x2_send.at[0], x2_recv.at[0], at_x(2)
-    )
-    far_first.start()
-    own_copies = [
-        pltpu.make_async_copy(
-            wq_hbm.at[:, c], wg.at[:, x, z, c], own_sem.at[0]
-        ),
-        pltpu.make_async_copy(wo_hbm.at[:, lanes], owg.at[x, z, :, lanes], own_sem.at[1]),
-        pltpu.make_async_copy(lw_hbm, lwg.at[r], own_sem.at[2]),
-    ]
-    for copy in own_copies:
-        copy.start()
-
-    gain = norm_gain[...]
-
-    @pl.loop(0, F // C)
-    def _(i):
-        rows = pl.ds(pl.multiple_of(i * C, C), C)
-        v = frames[rows, :].astype(F32)
-        centred = v - jnp.mean(v, axis=1, keepdims=True)
-        spread = jnp.mean(centred * centred, axis=1, keepdims=True)
-        normed = (centred * lax.rsqrt(spread + EPS_NORM) * gain).astype(BF)
-        xs[rows, :] = normed
-        start = first_frame + i * C
-        live = start + lax.broadcasted_iota(jnp.int32, (C, 1), 0) < length
-        total = jnp.sum(jnp.where(live, normed.astype(F32), 0.0), axis=0, keepdims=True)
-        count = jnp.clip(length - start, 1, C).astype(F32)
-        mrows[pl.ds(i, 1), :] = total / count
-
-    means = mrows[...]
-    power = jnp.mean(means * means, axis=1, keepdims=True)
-    mg[x, z] = (means * lax.rsqrt(power + EPS_MEMORY) * memory_gain[...]).astype(BF)
-
-    def round_one(v):
-        ring_next(v, 1)
-        across_start(mg.at[x, z], mg.at[x, z], xm_send, xm_recv, (1, 3, 2))
-        if v == 0:
-            ring_start(1, m_ring(v), zm_send, zm_recv)
-
-    def ring_next(v, k):
-        ring_wait(k, w_ring(v, 0), zw_send, zw_recv)
-        if k < ZK:
-            ring_start(k + 1, w_ring(v, 0), zw_send, zw_recv)
-        else:
-            to_sibling(v, 0).start()
-        for o in arrived(k):
-            across_start(w_ring(v, 0)(o), w_ring(v, 0)(o), xw_send, xw_recv, (1, 3))
-
-    def memory_next(v, k):
-        ring_wait(k, m_ring(v), zm_send, zm_recv)
-        if k < ZK:
-            ring_start(k + 1, m_ring(v), zm_send, zm_recv)
-        if v == 0:
-            for o in arrived(k):
-                across_start(mg.at[x, o], mg.at[x, o], xm_send, xm_recv, (1, 3, 2))
-
-    for copy in own_copies:
-        copy.wait()
-    per_core(round_one)
-
-    right = remote(
-        xs.at[pl.ds(0, 16)], xs.at[pl.ds(F, 16)], r_send.at[0], r_recv.at[0], (r, wrap(t - 1, N_TM))
-    )
-    right.start()
-
-    def o_z(o):
-        return owg.at[x, o, :, lanes]
-
-    def o_x(e):
-        return owg.at[group(e), :, :, lanes]
-
-    def o_y(by, core):
-        return owg.at[:, :, :, pl.ds(pl.multiple_of((wrap(y - by, NY) * 2 + core) * 128, 128), 128)]
-
-    for d in range(1, NZ):
-        remote(o_z(z), o_z(z), oz_send.at[d], oz_recv.at[d], at_z(d)).start()
-
-    def out_across():
-        for d in range(1, NZ):
-            ref = o_z(wrap(z - d, NZ))
-            remote(ref, ref, oz_send.at[d], oz_recv.at[d], at_z(d)).wait_recv()
-        for e in (1, 3, 2):
-            remote(o_x(0), o_x(0), ox_send.at[e], ox_recv.at[e], at_x(e)).start()
-
-    def out_up():
-        for e in (1, 3, 2):
-            remote(o_x(e), o_x(e), ox_send.at[e], ox_recv.at[e], at_x(e)).wait_recv()
-        for by in (1, 3, 2):
-            remote(o_y(0, c), o_y(0, c), oy_send.at[by], oy_recv.at[by], at_y(by)).start()
-        remote(o_y(0, c), o_y(0, c), os_send.at[0], os_recv.at[0], sib).start()
-
-    def out_side():
-        for by in (1, 3, 2):
-            ref = o_y(by, c)
-            remote(ref, ref, oy_send.at[by], oy_recv.at[by], at_y(by)).wait_recv()
-            remote(ref, ref, os_send.at[by], os_recv.at[by], sib).start()
-
-    def out_end():
-        for by in range(NY):
-            ref = o_y(by, 1 - c)
-            remote(ref, ref, os_send.at[by], os_recv.at[by], sib).wait_recv()
-
-    lw_up, lw_down, lw_far = (wrap(y + k, NY) * 2 + c for k in (1, -1, 2))
-
-    def lw_half(slot, d):
-        return lwg.at[slot, pl.ds(d * (D // 2), D // 2)]
-
-    def hop(ref, k, device=sib):
-        return remote(ref, ref, l_send.at[k], l_recv.at[k], device)
-
-    def side(ref, k):
-        return remote(ref, ref, ls_send.at[k], ls_recv.at[k], sib)
-
-    hop(lwg.at[r], 0, at_y(1)).start()
-    hop(lwg.at[r], 1, at_y(-1)).start()
-    side(lwg.at[r], 0).start()
-
-    def lw_step_two():
-        hop(lwg.at[lw_down], 0).wait_recv()
-        hop(lwg.at[lw_up], 1).wait_recv()
-        hop(lw_half(lw_down, 0), 2, at_y(1)).start()
-        hop(lw_half(lw_up, 1), 3, at_y(-1)).start()
-        side(lwg.at[lw_down], 1).start()
-        side(lwg.at[lw_up], 2).start()
-
-    def lw_step_three():
-        hop(lw_half(lw_far, 0), 2).wait_recv()
-        hop(lw_half(lw_far, 1), 3).wait_recv()
-        side(lwg.at[lw_far], 3).start()
-
     span0 = t * (F // C)
 
     @pl.loop(0, F // QB)
@@ -334,6 +112,231 @@
     kk[pl.ds(MEM + F, QB), :] = jnp.zeros((QB, GW), BF)
     vv[pl.ds(MEM + F, QB), :] = jnp.zeros((QB, GW), BF)
 
+    pl.semaphore_wait(barrier, N_TM - 1 + 2 * NY - 1)
+
+    def remote(src, dst, send, recv, device):
+        return pltpu.make_async_remote_copy(
+            src_ref=src,
+            dst_ref=dst,
+            send_sem=send,
+            recv_sem=recv,
+            device_id=device,
+            device_id_type=pl.DeviceIdType.MESH,
+        )
+
+    def at_z(by):
+        return (r, x * NZ + wrap(z + by, NZ))
+
+    def at_x(by):
+        return (r, wrap(x + by, NX) * NZ + z)
+
+    def at_y(by):
+        return (wrap(y + by, NY) * 2 + c, t)
+
+    def per_core(fn):
+        for v in (0, 1):
+            pl.when(c == v)(functools.partial(fn, v))
+
+    ZK = NZ // 2
+
+    def halved(ref, k, d):
+        if k < ZK:
+            return ref
+        return ref.at[(slice(None),) * (len(ref.shape) - 1) + (pl.ds(d * (D // 2), D // 2),)]
+
+    def ring_start(k, piece, send, recv, own=None):
+        for d, s in enumerate((1, -1)):
+            dst = halved(piece(wrap(z - s * (k - 1), NZ)), k, d)
+            n = 2 * (k - 1) + d
+            remote(own if own is not None else dst, dst, send.at[n], recv.at[n], at_z(s)).start()
+
+    def ring_wait(k, piece, send, recv):
+        for d, s in enumerate((1, -1)):
+            ref = halved(piece(wrap(z - s * k, NZ)), k, d)
+            n = 2 * (k - 1) + d
+            copy = remote(ref, ref, send.at[n], recv.at[n], at_z(s))
+            copy.wait_recv()
+            copy.wait_send()
+
+    def arrived(k):
+        return [wrap(z - k, NZ)] + ([wrap(z + k, NZ)] if k < ZK else [])
+
+    def group(e):
+        return wrap(x - e, NX)
+
+    def w_ring(v, e):
+        return lambda o: wg.at[:, group(e), o, v]
+
+    def w_group(v, e):
+        return wg.at[:, group(e), :, v]
+
+    def m_ring(v):
+        return (lambda o: mg.at[x, o]) if v == 0 else (lambda o: mg.at[:, o])
+
+    def across_start(src, dst, send, recv, peers):
+        for e in peers:
+            remote(src, dst, send.at[e], recv.at[e], at_x(e)).start()
+
+    def w_across(v, e):
+        return w_group(v, e)
+
+    def m_across(v, e):
+        return mg.at[group(e)] if v == 0 else mg.at[group(e), z]
+
+    def across_wait(ref, recv, e):
+        remote(ref, ref, xw_send.at[e], recv.at[e], at_x(e)).wait_recv()
+
+    def to_sibling(v, e):
+        return remote(w_group(v, e), w_group(v, e), sw_send.at[e], sw_recv.at[e], sib)
+
+    def from_sibling(e):
+        def wait(v):
+            to_sibling(1 - v, e).wait_recv()
+
+        per_core(wait)
+
+    lanes = pl.ds(pl.multiple_of(r * 128, 128), 128)
+
+    def first_hop(v):
+        own = wq_hbm.at[:, v]
+        ring_start(1, w_ring(v, 0), zw_send, zw_recv, own=own)
+        across_start(own, wg.at[:, x, z, v], xw_send, xw_recv, (1, 3))
+
+    per_core(first_hop)
+    far_first = remote(
+        wq_hbm.at[:, :, :, lanes], wg.at[:, x, z, :, :, lanes], x2_send.at[0], x2_recv.at[0], at_x(2)
+    )
+    far_first.start()
+    for d in range(1, NZ):
+        remote(
+            wo_hbm.at[:, lanes], owg.at[x, z, :, lanes], oz_send.at[d], oz_recv.at[d], at_z(d)
+        ).start()
+    own_copies = [
+        pltpu.make_async_copy(
+            wq_hbm.at[:, c], wg.at[:, x, z, c], own_sem.at[0]
+        ),
+        pltpu.make_async_copy(wo_hbm.at[:, lanes], owg.at[x, z, :, lanes], own_sem.at[1]),
+        pltpu.make_async_copy(lw_hbm, lwg.at[r], own_sem.at[2]),
+    ]
+    for copy in own_copies:
+        copy.start()
+
+    gain = norm_gain[...]
+
+    @pl.loop(0, F // C)
+    def _(i):
+        rows = pl.ds(pl.multiple_of(i * C, C), C)
+        v = frames[rows, :].astype(F32)
+        centred = v - jnp.mean(v, axis=1, keepdims=True)
+        spread = jnp.mean(centred * centred, axis=1, keepdims=True)
+        normed = (centred * lax.rsqrt(spread + EPS_NORM) * gain).astype(BF)
+        xs[rows, :] = normed
+        start = first_frame + i * C
+        live = start + lax.broadcasted_iota(jnp.int32, (C, 1), 0) < length
+        total = jnp.sum(jnp.where(live, normed.astype(F32), 0.0), axis=0, keepdims=True)
+        count = jnp.clip(length - start, 1, C).astype(F32)
+        mrows[pl.ds(i, 1), :] = total / count
+
+    means = mrows[...]
+    power = jnp.mean(means * means, axis=1, keepdims=True)
+    mg[x, z] = (means * lax.rsqrt(power + EPS_MEMORY) * memory_gain[...]).astype(BF)
+
+    def round_one(v):
+        ring_next(v, 1)
+        across_start(mg.at[x, z], mg.at[x, z], xm_send, xm_recv, (1, 3, 2))
+        if v == 0:
+            ring_start(1, m_ring(v), zm_send, zm_recv)
+
+    def ring_next(v, k):
+        ring_wait(k, w_ring(v, 0), zw_send, zw_recv)
+        if k < ZK:
+            ring_start(k + 1, w_ring(v, 0), zw_send, zw_recv)
+        else:
+            to_sibling(v, 0).start()
+        for o in arrived(k):
+            across_start(w_ring(v, 0)(o), w_ring(v, 0)(o), xw_send, xw_recv, (1, 3))
+
+    def memory_next(v, k):
+        ring_wait(k, m_ring(v), zm_send, zm_recv)
+        if k < ZK:
+            ring_start(k + 1, m_ring(v), zm_send, zm_recv)
+        if v == 0:
+            for o in arrived(k):
+                across_start(mg.at[x, o], mg.at[x, o], xm_send, xm_recv, (1, 3, 2))
+
+    for copy in own_copies:
+        copy.wait()
+    per_core(round_one)
+
+    right = remote(
+        xs.at[pl.ds(0, 16)], xs.at[pl.ds(F, 16)], r_send.at[0], r_recv.at[0], (r, wrap(t - 1, N_TM))
+    )
+    right.start()
+
+    def o_z(o):
+        return owg.at[x, o, :, lanes]
+
+    def o_x(e):
+        return owg.at[group(e), :, :, lanes]
+
+    def o_y(by, core):
+        return owg.at[:, :, :, pl.ds(pl.multiple_of((wrap(y - by, NY) * 2 + core) * 128, 128), 128)]
+
+    def out_across():
+        for d in range(1, NZ):
+            ref = o_z(wrap(z - d, NZ))
+            remote(ref, ref, oz_send.at[d], oz_recv.at[d], at_z(d)).wait_recv()
+        for e in (1, 3, 2):
+            remote(o_x(0), o_x(0), ox_send.at[e], ox_recv.at[e], at_x(e)).start()
+
+    def out_up():
+        for e in (1, 3, 2):
+            remote(o_x(e), o_x(e), ox_send.at[e], ox_recv.at[e], at_x(e)).wait_recv()
+        for by in (1, 3, 2):
+            remote(o_y(0, c), o_y(0, c), oy_send.at[by], oy_recv.at[by], at_y(by)).start()
+        remote(o_y(0, c), o_y(0, c), os_send.at[0], os_recv.at[0], sib).start()
+
+    def out_side():
+        for by in (1, 3, 2):
+            ref = o_y(by, c)
+            remote(ref, ref, oy_send.at[by], oy_recv.at[by], at_y(by)).wait_recv()
+            remote(ref, ref, os_send.at[by], os_recv.at[by], sib).start()
+
+    def out_end():
+        for by in range(NY):
+            ref = o_y(by, 1 - c)
+            remote(ref, ref, os_send.at[by], os_recv.at[by], sib).wait_recv()
+
+    out_across()
+
+    lw_up, lw_down, lw_far = (wrap(y + k, NY) * 2 + c for k in (1, -1, 2))
+
+    def lw_half(slot, d):
+        return lwg.at[slot, pl.ds(d * (D // 2), D // 2)]
+
+    def hop(ref, k, device=sib):
+        return remote(ref, ref, l_send.at[k], l_recv.at[k], device)
+
+    def side(ref, k):
+        return remote(ref, ref, ls_send.at[k], ls_recv.at[k], sib)
+
+    hop(lwg.at[r], 0, at_y(1)).start()
+    hop(lwg.at[r], 1, at_y(-1)).start()
+    side(lwg.at[r], 0).start()
+
+    def lw_step_two():
+        hop(lwg.at[lw_down], 0).wait_recv()
+        hop(lwg.at[lw_up], 1).wait_recv()
+        hop(lw_half(lw_down, 0), 2, at_y(1)).start()
+        hop(lw_half(lw_up, 1), 3, at_y(-1)).start()
+        side(lwg.at[lw_down], 1).start()
+        side(lwg.at[lw_up], 2).start()
+
+    def lw_step_three():
+        hop(lw_half(lw_far, 0), 2).wait_recv()
+        hop(lw_half(lw_far, 1), 3).wait_recv()
+        side(lwg.at[lw_far], 3).start()
+
     def round_two(v):
         if v == 1:
             for e in (1, 3, 2):
@@ -408,7 +411,6 @@
             remote(ref, ref, s2_send.at[by], s2_recv.at[by], sib).wait_recv()
 
     per_core(round_two)
-    out_across()
     per_core(round_three)
     per_core(round_four)
     out_up()

time: 84.5 us -> 83.2 us (0.985)
  Pallas kernels: 79.7 us -> 78.4 us
    pallas_call x1, Pallas kernels: 79.7 us -> 78.4 us  [per_device(): pl.pallas_call(kernel, out_shape=(jax.ShapeDtypeStruct((F, D), BF), jax.S...]
where the time goes in v4:
time: 83.2 us; the launch traced here: 83 us
  Pallas kernels  78.4 us (94%)
  local copies, waits for them, and re-layouts  3.32 us (4%)
  between operations  1.29 us (2%)
    pallas_call x1, Pallas kernels, per_device(): pl.pallas_call(kernel, out_shape=(jax.ShapeDtypeStruct((F, D), BF), jax.S...  78.4 us
    unnamed x4, local copies, waits for them, and re-layouts  3.32 us

profile of v4, /device:TPU:1, one launch (start us, length us, event | category | flops | bytes accessed | tf_op | source)
XLA Modules:
  0.0 83.0 jit_solution(17311701614567921077)
XLA Ops:
  1.3 78.4 %block.1 = (bf16[512,1024]{1,0:T(8,128)(2,1)}, bf16[256,2048]{1,0:T(8,128)(2,1)}) custom-call(bf16[512,1024]{1,0:T(8,128)(2,1)} %bitcast.11, s32[1]{0:T(128)S(6)} %copy.13.lengths, f32[1,1024]{1,0:T(1,128)} %bitcast.16, f32[1,1024]{1,0:T(1,128)} %bitcast.17, bf16[3,2,16,1024]{3,2,1,0:T(8,128)(2,1)} %bitcast.14, bf16[32,1024]{1,0:T(8,128)(2,1)} %bitcast.15, ...), custom_call_target="tpu_custom_call" | custom-call | tf_op jit(solution)/shard_map/block/pallas_call | solution.py:604
  79.7 0.0 copy-start
  79.7 2.4 %copy.14 = bf16[1,512,1024]{2,1,0:T(8,128)(2,1)} copy(bf16[1,512,1024]{2,1,0:T(8,128)(2,1)} %bitcast.13) | data formatting | bytes 2097152
  82.0 0.0 copy-done
  82.0 1.0 %copy.15 = bf16[1,1,256,2048]{3,2,1,0:T(8,128)(2,1)} copy(bf16[1,1,256,2048]{3,2,1,0:T(8,128)(2,1)S(1)} %bitcast.12) | data formatting | bytes 2097152
Async XLA Ops:
  79.7 2.4 %copy-start = (bf16[256,2048]{1,0:T(8,128)(2,1)S(1)}, bf16[256,2048]{1,0:T(8,128)(2,1)}, u32[]{:S(2)}) copy-start(bf16[256,2048]{1,0:T(8,128)(2,1)} %get-tuple-element.5) | copy-start | bytes 3145732

commit v5 on v4

--- a/solution.py
+++ b/solution.py
@@ -28,7 +28,7 @@
 QB = 64
 MEM = N_TM * F // C
 KW = MEM + 2 * QB
-NCH = 2
+NCH = 1
 CH = D // NCH
 LOG2E = 1.4426950408889634
 BF = jnp.bfloat16
@@ -412,8 +412,8 @@
 
     per_core(round_two)
     per_core(round_three)
+    out_up()
     per_core(round_four)
-    out_up()
     far_along()
     per_core(round_five)
     from_sibling(0)

time: 83.2 us -> 83.4 us (level)
  no operation moved by 1% of the time
where the time goes in v5:
time: 83.4 us; the launch traced here: 83.2 us
  Pallas kernels  78.6 us (94%)
  local copies, waits for them, and re-layouts  3.32 us (4%)
  between operations  1.29 us (2%)
    pallas_call x1, Pallas kernels, per_device(): pl.pallas_call(kernel, out_shape=(jax.ShapeDtypeStruct((F, D), BF), jax.S...  78.6 us
    unnamed x4, local copies, waits for them, and re-layouts  3.32 us

profile of v5, /device:TPU:1, one launch (start us, length us, event | category | flops | bytes accessed | tf_op | source)
XLA Modules:
  0.0 83.2 jit_solution(11558886061119336862)
XLA Ops:
  1.3 78.6 %block.1 = (bf16[512,1024]{1,0:T(8,128)(2,1)}, bf16[256,2048]{1,0:T(8,128)(2,1)}) custom-call(bf16[512,1024]{1,0:T(8,128)(2,1)} %bitcast.11, s32[1]{0:T(128)S(6)} %copy.13.lengths, f32[1,1024]{1,0:T(1,128)} %bitcast.16, f32[1,1024]{1,0:T(1,128)} %bitcast.17, bf16[3,2,16,1024]{3,2,1,0:T(8,128)(2,1)} %bitcast.14, bf16[32,1024]{1,0:T(8,128)(2,1)} %bitcast.15, ...), custom_call_target="tpu_custom_call" | custom-call | tf_op jit(solution)/shard_map/block/pallas_call | solution.py:604
  79.9 0.0 copy-start
  79.9 2.4 %copy.14 = bf16[1,512,1024]{2,1,0:T(8,128)(2,1)} copy(bf16[1,512,1024]{2,1,0:T(8,128)(2,1)} %bitcast.13) | data formatting | bytes 2097152
  82.3 0.0 copy-done
  82.3 1.0 %copy.15 = bf16[1,1,256,2048]{3,2,1,0:T(8,128)(2,1)} copy(bf16[1,1,256,2048]{3,2,1,0:T(8,128)(2,1)S(1)} %bitcast.12) | data formatting | bytes 2097152
Async XLA Ops:
  79.9 2.4 %copy-start = (bf16[256,2048]{1,0:T(8,128)(2,1)S(1)}, bf16[256,2048]{1,0:T(8,128)(2,1)}, u32[]{:S(2)}) copy-start(bf16[256,2048]{1,0:T(8,128)(2,1)} %get-tuple-element.5) | copy-start | bytes 3145732
